TPU v7x, 256 devices: a whole 4x4x8 slice. The times are simulated.
256 devices in a mesh: re: 8 (over x, y_lo), rp: 16 (over z, core), mode: 2 (over y_hi).
Axes of the slice: x: 4, y: 4 (y_hi: 2, y_lo: 2; y = y_hi * 2 + y_lo), z: 8, core: 2. Of those that a mesh axis runs over, the one named last changes fastest.
Arguments:
- coupling: float32 [2, 64, 16, 120, 576], P(None, 're', 'rp', 'mode'), may hold values from -0.1875 to 0.1875
- electron_cells: int32 [64, 3], replicated, may hold values from -6 to 6
- phonon_cells: int32 [16, 3], replicated, may hold values from -3 to 3
- kpoint_index: int32 [16, 3], replicated, may hold values from 0 to 15
- qpoint_index: int32 [16, 3], replicated, may hold values from 0 to 15
- eigenvectors: float32 [16, 2, 120, 120], P('rp', None, 'mode'), may hold values from -0.5 to 0.5
- frequencies: float32 [16, 120], P('rp', 'mode'), may hold values from 0.25 to 2
Outputs:
- mode_coupling: float32 [120, 16, 16, 2, 576], P('mode', 'rp', 're')
All inputs are finite; a program needn't handle non-finite values.
Results may differ from a plain program's by a relative error of at most 0.00007.
Values sent between devices are 32-bit elements; how exact they have to be, the bound alone decides.
No kernel may reach another device: no remote copies, remote signals or barrier semaphores. Data moves between devices by JAX's collectives and lax.ppermute only.
A program may use at most 64 MiB of HBM per device.

v0:
```python
import jax
import jax.numpy as jnp
from jax import lax
from jax.sharding import PartitionSpec as P

KG = 16


def cut_along(shard, dim, length):
    dims = shard.shape
    parts = shard.reshape(*dims[:dim], length, dims[dim] // length, *dims[dim + 1 :])
    return jnp.moveaxis(parts, dim, 0)


def sum_at_owner(shard, axis, dim):
    parts = cut_along(shard, dim, lax.axis_size(axis))
    arrived = lax.all_to_all(parts, axis, split_axis=0, concat_axis=0, tiled=True)
    return arrived.sum(axis=0)


def phases(points, cells):
    turns = jnp.sum(points[:, None, :] * cells[None, :, :], axis=-1) % KG
    angle = turns.astype(jnp.float32) * (2.0 * 3.141592653589793 / KG)
    return (jnp.cos(angle), jnp.sin(angle))


def complex_rows(cos_t, sin_t):
    count = cos_t.shape[0]
    upper = jnp.stack([cos_t, -sin_t], axis=1)
    lower = jnp.stack([sin_t, cos_t], axis=1)
    return jnp.stack([upper, lower], axis=1).reshape(count * 2, 2 * cos_t.shape[1])


def electron_apply(cos_t, sin_t, block):
    rows = block.shape[1]
    rest = block.shape[2:]
    flat = block.reshape(2 * rows, -1)
    summed = jnp.dot(complex_rows(cos_t, sin_t), flat, precision=lax.Precision.HIGHEST)
    return summed.reshape((cos_t.shape[0], 2) + rest)


def phonon_apply(cos_t, sin_t, block):
    hp = lax.Precision.HIGHEST
    swapped = jnp.concatenate([-block[:, 1:2], block[:, 0:1]], axis=1)
    first_term = jnp.einsum("qs,kbsx->qkbx", cos_t, block, precision=hp)
    second_term = jnp.einsum("qs,kbsx->qkbx", sin_t, swapped, precision=hp)
    return first_term + second_term


def shards(
    coupling, electron_cells, phonon_cells, kpoint_index, qpoint_index, eigenvectors, frequencies
):
    hp = lax.Precision.HIGHEST
    re_local = coupling.shape[1]
    rp_local = coupling.shape[2]
    modes_local = coupling.shape[3]
    pairs = coupling.shape[4]
    k_local = kpoint_index.shape[0] // lax.axis_size("re")
    q_local = qpoint_index.shape[0] // lax.axis_size("rp")
    columns = coupling.reshape(2, re_local, rp_local, modes_local * pairs)
    my_electron = lax.dynamic_slice_in_dim(
        electron_cells, lax.axis_index("re") * re_local, re_local, 0
    )
    points = kpoint_index
    cos_e, sin_e = phases(points, my_electron)
    bloch_k = lax.psum_scatter(
        electron_apply(cos_e, sin_e, columns), "re", scatter_dimension=0, tiled=True
    )
    my_phonon = lax.dynamic_slice_in_dim(phonon_cells, lax.axis_index("rp") * rp_local, rp_local, 0)
    points = qpoint_index
    cos_p, sin_p = phases(points, my_phonon)
    bloch_kq = lax.psum_scatter(
        phonon_apply(cos_p, sin_p, bloch_k), "rp", scatter_dimension=0, tiled=True
    )
    bloch_kq = bloch_kq.reshape(q_local, k_local, 2, modes_local, pairs)
    contract = (((0,), (2,)), ((), ()))
    kq_one = bloch_kq[0]
    swapped = jnp.concatenate([-kq_one[:, 1:2], kq_one[:, 0:1]], axis=1)
    vec_real = eigenvectors[0, 0]
    vec_imag = eigenvectors[0, 1]
    part_one = lax.dot_general(vec_real, kq_one, contract, precision=hp)
    part_two = lax.dot_general(vec_imag, swapped, contract, precision=hp)
    results = [part_one + part_two]
    rotated = sum_at_owner(jnp.stack(results, axis=1), "mode", 0)
    factor = lax.rsqrt(2.0 * frequencies).T[:, :, None, None, None]
    return rotated * factor


def solution(mesh):
    placed = (
        P(None, "re", "rp", "mode", None),
        P(),
        P(),
        P(),
        P(),
        P("rp", None, "mode", None),
        P("rp", "mode"),
    )
    return jax.shard_map(
        shards,
        mesh=mesh,
        in_specs=placed,
        out_specs=P("mode", "rp", "re", None, None),
        check_vma=False,
    )
```

profile of v0, /device:TPU:1, one launch (start us, length us, event | category | flops | bytes accessed | tf_op | source)
XLA Modules:
  0.0 408.9 jit_solution(4533368896630028435)
XLA Ops:
  6.5 0.7 copy-done
  7.2 0.1 constant_dynamic-slice_fusion.2
  7.3 0.8 multiply_reduce_fusion
  8.0 0.1 fusion.18
  8.1 0.1 copy.35
  8.2 0.1 copy.36
  8.3 7.8 %reduce.4 = f32[2,8,60,576]{3,2,1,0:T(8,128)S(1)} reduce(f32[2,8,1,60,576]{4,2,3,1,0:T(1,128)} %param.7, f32[]{:T(128)} %constant.59), dimensions={2}, to_apply=%param.7.reduce_sub_computation | reduce | bytes 4423684 | tf_op args[0]
  16.1 2.2 reshape.133
  18.3 6.9 %convolution_bitcast_fusion = f32[16,2,1,34560]{3,0,1,2:T(8,128)} fusion(f32[16,34560,1]{1,0,2:T(8,128)} %reshape.133, f32[16,1,16]{2,0,1:T(8,128)S(1)} %copy.36, f32[16,1,16]{2,0,1:T(8,128)S(1)} %copy.35), kind=kOutput, calls=%fused_computation | convolution fusion | flops 212337152 | bytes 6637568 | tf_op jit(solution)/shard_map/dot_general | solution.py:38
  25.2 0.2 all-reduce.7.cloned.1.call-start
  25.5 0.2 dynamic-slice_reduce_fusion
  25.7 0.1 multiply_reduce_fusion.1
  25.9 0.6 dynamic-slice
  27.1 197.7 %all-reduce.5.cloned.1.call-done = f32[16,2,1,34560]{3,0,1,2:T(8,128)} async-done(((f32[16,2,1,34560]{3,0,1,2:T(8,128)}), f32[16,2,1,34560]{3,0,1,2:T(8,128)}) %all-reduce.5.cloned.1.call-update) | async-done | bytes 4423696
  224.8 1.8 dynamic-slice_negate_fusion
  226.6 0.2 maximum_bitcast_fusion
  226.9 0.3 copy.38
  227.2 1.8 dynamic-slice_bitcast_fusion
  229.0 0.3 copy.37
  229.3 7.1 %multiply_add_fusion = f32[16,2,2,34560]{3,2,1,0:T(2,128)} fusion(f32[2,2,34560]{2,1,0:T(2,128)S(1)} %copy.38, f32[2,2,34560]{2,1,0:T(2,128)S(1)} %copy.37, f32[16]{0:T(128)S(1)} %sin.25, f32[16]{0:T(128)S(1)} %get-tuple-element.5), kind=kLoop, calls=%fused_computation.1 | loop fusion | flops 6635520 | bytes 9953408 | tf_op jit(solution)/shard_map/add | solution.py:47
  236.5 0.7 copy-done.5
  237.1 0.6 dynamic-slice.2
  237.8 135.3 %all-reduce.7.cloned.1.call-done = f32[16,2,2,34560]{3,2,1,0:T(2,128)} async-done(((f32[16,2,2,34560]{3,2,1,0:T(2,128)}), f32[16,2,2,34560]{3,2,1,0:T(2,128)}) %all-reduce.7.cloned.1.call-update) | async-done | bytes 8847376
  373.1 1.7 constant_dynamic-slice_fusion.1
  374.8 0.6 squeeze_reshape.3
  375.5 2.0 fusion.4
  377.5 2.0 fusion
  379.5 1.5 copy.41
  381.0 4.0 all-to-all-start
  385.0 14.8 %all-to-all-done = f32[2,60,1,2,2,576]{5,4,3,1,2,0:T(2,128)S(1)} async-done(((f32[2,60,1,2,2,576]{5,4,3,1,2,0:T(2,128)}), f32[2,60,1,2,2,576]{5,4,3,1,2,0:T(2,128)S(1)}, u32[]{:S(2)}, u32[]{:S(2)}) %all-to-all-start) | async-done | bytes 1105952 | tf_op jit(solution)/shard_map/all_to_all | solution.py:17
  399.8 1.2 reduce_sum.34
  401.0 1.1 bitcast_multiply_fusion
  (21 shorter events, 0.3 us)
Async XLA Ops:
  6.5 0.7 copy-start
  6.5 218.3 %all-reduce.5.cloned.1.call-start = ((), (), s32[]{:S(2)}) async-start(), calls=%async_computation.1 | async-start | bytes 8847360
  18.3 7.2 %copy-start.2 = (s32[16,3]{0,1:T(4,128)S(1)}, s32[16,3]{0,1:T(4,128)}, u32[]{:S(2)}) copy-start(s32[16,3]{0,1:T(4,128)} %param.9) | copy-start | bytes 580
  18.3 7.4 %copy-start.3 = (s32[16,3]{0,1:T(4,128)S(1)}, s32[16,3]{0,1:T(4,128)}, u32[]{:S(2)}) copy-start(s32[16,3]{0,1:T(4,128)} %param.11) | copy-start | bytes 580
  18.3 7.6 %copy-start.6 = (u32[256]{0:T(256)S(1)}, u32[256]{0:T(256)}, u32[]{:S(2)}) copy-start(u32[256]{0:T(256)} %constant.52) | copy-start | bytes 3076
  25.2 347.9 %all-reduce.7.cloned.1.call-start = ((), (), s32[]{:S(2)}) async-start(), calls=%async_computation.2 | async-start | bytes 17694720
  236.4 0.7 copy-start.5
  236.4 1.3 copy-start.1
  377.5 7.5 %copy-start.4 = (f32[1,60]{1,0:T(1,128)S(1)}, f32[1,60]{1,0:T(1,128)}, u32[]{:S(2)}) copy-start(f32[1,60]{1,0:T(1,128)} %param.13) | copy-start | bytes 724
  381.0 18.8 %all-to-all-start = ((f32[2,60,1,2,2,576]{5,4,3,1,2,0:T(2,128)}), f32[2,60,1,2,2,576]{5,4,3,1,2,0:T(2,128)S(1)}, u32[]{:S(2)}, u32[]{:S(2)}) async-start(f32[2,60,1,2,2,576]{5,4,3,1,2,0:T(2,128)} %bitcast.14), calls=%async_computation | async-start | bytes 2457600 | tf_op jit(solution)/shard_map/all_to_all | solution.py:17
Sparse Core Ops, SparseCore 0:
  25.3 199.4 all-reduce.4
  236.6 136.4 all-reduce.6
where the time goes:
time: 411 us; the launch traced here: 409 us
  waiting for transfers between devices  348 us (85%)
  other arithmetic  20.3 us (5%)
  between operations  14.2 us (3%)
  local copies, waits for them, and re-layouts  11.4 us (3%)
  matrix products  11 us (3%)
  starting transfers between devices  4.22 us (1%)
    unnamed x4, waiting for transfers between devices  333 us
    all_to_all x1, waiting for transfers between devices, sum_at_owner(): lax.all_to_all(parts, axis, split_axis=0, concat_axis=0, tiled=True)  14.8 us
  transfers between devices with their start and end apart: 3, of which 3 were waited for; matrix products, arithmetic and copies ran while one was open for 0% of the time, Pallas kernels for 0%

commit v1 on v0

v1 whole, which is shorter than its diff:
```python
import jax
import jax.numpy as jnp
from jax import lax
from jax.sharding import PartitionSpec as P

KG = 16
HP = lax.Precision.HIGHEST
LANES = 128


def phases(points, cells):
    turns = jnp.sum(points[:, None, :] * cells[None, :, :], axis=-1) % KG
    angle = turns.astype(jnp.float32) * (2.0 * 3.141592653589793 / KG)
    return (jnp.cos(angle), jnp.sin(angle))


def rotation(points, cells):
    cos_t, sin_t = phases(points, cells)
    upper = jnp.stack([cos_t, -sin_t], axis=-1)
    lower = jnp.stack([sin_t, cos_t], axis=-1)
    return jnp.stack([upper, lower], axis=1)


def exchange(parts, axis):
    return lax.all_to_all(parts, axis, split_axis=0, concat_axis=0, tiled=True)


def shards(
    coupling, electron_cells, phonon_cells, kpoint_index, qpoint_index, eigenvectors, frequencies
):
    re_size = lax.axis_size("re")
    rp_size = lax.axis_size("rp")
    _, re_local, _, modes_local, pairs = coupling.shape
    nk = kpoint_index.shape[0]
    nq = qpoint_index.shape[0]
    nre = electron_cells.shape[0]
    nrp = phonon_cells.shape[0]
    columns = modes_local * pairs
    piece = -(-columns // (re_size * LANES))
    padded = piece * re_size * LANES

    scale = lax.rsqrt(2.0 * frequencies[0])
    mine = lax.axis_index("mode")
    other_vec = lax.ppermute(eigenvectors[0], "mode", [(0, 1), (1, 0)])
    other_scale = lax.ppermute(scale, "mode", [(0, 1), (1, 0)])
    pair_vec = jnp.stack([eigenvectors[0], other_vec])
    vec = jnp.where(mine == 0, pair_vec, pair_vec[::-1])
    vec = jnp.moveaxis(vec, 0, 1).reshape(2, 2 * modes_local, -1)
    pair_scale = jnp.stack([scale, other_scale])
    scales = jnp.where(mine == 0, pair_scale, pair_scale[::-1]).reshape(-1)
    vec = vec * scales[None, None, :]

    flat = coupling.reshape(2, re_local, columns)
    flat = jnp.pad(flat, ((0, 0), (0, 0), (0, padded - columns)))
    flat = flat.reshape(2, re_local, re_size, piece, LANES).transpose(2, 1, 0, 3, 4)
    got = exchange(flat, "re")
    rot_e = rotation(kpoint_index, electron_cells).reshape(nk * 2, nre * 2)
    bloch_k = jnp.einsum(
        "kr,rab->kab", rot_e, got.reshape(nre * 2, piece, LANES), precision=HP
    )

    got = exchange(bloch_k.reshape(nk, 2, piece, LANES), "rp")
    rot_p = rotation(qpoint_index, phonon_cells).reshape(nq * 2, nrp * 2)
    bloch_kq = jnp.einsum(
        "qs,sab->qab", rot_p, got.reshape(nrp * 2, piece, LANES), precision=HP
    )

    got = exchange(bloch_kq.reshape(nq, 2, piece, LANES), "rp")
    got = exchange(got, ("re", "mode"))
    got = got.reshape(re_size, 2, 2, piece, LANES).transpose(2, 1, 0, 3, 4)
    got = got.reshape(2, 2, padded)[:, :, :columns].reshape(2, 2 * modes_local, pairs)

    real = jnp.stack([vec[0], -vec[1]])
    imag = jnp.stack([vec[1], vec[0]])
    matrix = jnp.stack([real, imag])

    def rotate(start):
        half = lax.dynamic_slice_in_dim(matrix, start * modes_local, modes_local, 3)
        return jnp.einsum("gbcn,bcp->ngp", half, got, precision=HP)

    theirs = lax.ppermute(rotate(1 - mine), "mode", [(0, 1), (1, 0)])
    ours = rotate(mine)
    both = jnp.stack([ours, theirs], axis=1)
    both = jnp.where(mine == 0, both, both[:, ::-1])
    return both[:, None]


def solution(mesh):
    placed = (
        P(None, "re", "rp", "mode", None),
        P(),
        P(),
        P(),
        P(),
        P("rp", None, "mode", None),
        P("rp", "mode"),
    )
    return jax.shard_map(
        shards,
        mesh=mesh,
        in_specs=placed,
        out_specs=P("mode", "rp", "re", None, None),
        check_vma=False,
    )
```

time: 411 us -> 141 us (0.34)
  waiting for transfers between devices: 348 us -> 83.6 us
  starting transfers between devices: 4.22 us -> 28.7 us
  between operations: 14.2 us -> 0.24 us
  other arithmetic: 20.3 us -> 8.23 us
  matrix products: 11 us -> 3.03 us
  local copies, waits for them, and re-layouts: 11.4 us -> 16.3 us
    unnamed x4 -> x0, waiting for transfers between devices: 333 us -> none
    all_to_all x1 -> x4, waiting for transfers between devices: 14.8 us -> 70.9 us  [exchange(): return lax.all_to_all(parts, axis, split_axis=0, concat_axis=0, tiled=True)]
    all_to_all x1 -> x4, starting transfers between devices: 4 us -> 24.3 us  [exchange(): return lax.all_to_all(parts, axis, split_axis=0, concat_axis=0, tiled=True)]
    ppermute x0 -> x3, waiting for transfers between devices: none -> 12.6 us  [the longest x1 8.67 us: shards(): theirs = lax.ppermute(rotate(1 - mine), 'mode', [(0, 1), (1, 0)])]
    dot_general x3 -> x4, matrix products: 11 us -> 3.03 us  [the longest x1 1.22 us: shards(): jnp.einsum('kr,rab->kab', rot_e, got.reshape(nre * 2, piece, LANES), prec...]
    add x1 -> x0, other arithmetic: 7.14 us -> none  [phonon_apply(): return first_term + second_term]
    reshape x0 -> x6, local copies, waits for them, and re-layouts: none -> 5.06 us  [the longest x1 2.16 us: shards(): flat = coupling.reshape(2, re_local, columns)]
    another operation x7 -> x4, local copies, waits for them, and re-layouts: 5.3 us -> 0.3 us  [the longest x1 0.11 us: rotation(): upper = jnp.stack([cos_t, -sin_t], axis=-1)]
  transfers between devices with their start and end apart: 3 -> 7, of which waited for: 3 -> 6; matrix products, arithmetic and copies ran while one was open for 0% -> 1% of each run, Pallas kernels for 0% -> 0%
where the time goes in v1:
time: 141 us; the launch traced here: 140 us
  waiting for transfers between devices  83.6 us (59%)
  starting transfers between devices  28.7 us (20%)
  local copies, waits for them, and re-layouts  16.3 us (12%)
  other arithmetic  8.23 us (6%)
  matrix products  3.03 us (2%)
    all_to_all x4, waiting for transfers between devices, exchange(): return lax.all_to_all(parts, axis, split_axis=0, concat_axis=0, tiled=True)  70.9 us
    all_to_all x4, starting transfers between devices, exchange(): return lax.all_to_all(parts, axis, split_axis=0, concat_axis=0, tiled=True)  24.3 us
    ppermute x1, waiting for transfers between devices, shards(): theirs = lax.ppermute(rotate(1 - mine), 'mode', [(0, 1), (1, 0)])  8.67 us
    unnamed x1, other arithmetic  7.6 us
    ppermute x1, waiting for transfers between devices, shards(): other_scale = lax.ppermute(scale, 'mode', [(0, 1), (1, 0)])  3.97 us
    pad x1, local copies, waits for them, and re-layouts, shards(): flat = jnp.pad(flat, ((0, 0), (0, 0), (0, padded - columns)))  3.13 us
  transfers between devices with their start and end apart: 7, of which 6 were waited for; matrix products, arithmetic and copies ran while one was open for 1% of the time, Pallas kernels for 0%

profile of v1, /device:TPU:1, one launch (start us, length us, event | category | flops | bytes accessed | tf_op | source)
XLA Modules:
  0.0 140.0 jit_solution(6154734434028090405)
XLA Ops:
  0.0 7.6 %reduce = f32[2,8,60,576]{3,2,1,0:T(8,128)S(1)} reduce(f32[2,8,1,60,576]{4,2,3,1,0:T(1,128)} %param.7, f32[]{:T(128)} %constant.46), dimensions={2}, to_apply=%param.7.reduce_sub_computation | reduce | bytes 4423684 | tf_op args[0]
  7.6 2.2 %reshape.162 = f32[2,8,34560]{2,1,0:T(8,128)} reshape(f32[2,8,60,576]{3,2,1,0:T(8,128)S(1)} %reduce) | data formatting | bytes 4423680 | tf_op jit(solution)/shard_map/reshape | solution.py:53
  9.8 3.1 %pad.4 = f32[2,8,34816]{2,1,0:T(8,128)} pad(f32[2,8,34560]{2,1,0:T(8,128)} %reshape.162, f32[]{:T(128)} %constant.36.clone.1), padding=0_0x0_0x0_256 | pad | bytes 4440068 | tf_op jit(solution)/shard_map/jit(_pad)/pad | solution.py:54
  12.9 1.8 %reshape.163 = f32[2,8,8,34,128]{4,3,2,1,0:T(8,128)S(1)} reshape(f32[2,8,34816]{2,1,0:T(8,128)} %pad.4) | data formatting | bytes 4456448 | tf_op jit(solution)/shard_map/reshape | solution.py:55
  14.7 2.7 %copy.75 = f32[8,8,2,34,128]{4,1,3,2,0:T(8,128)} copy(f32[8,8,2,34,128]{4,3,0,1,2:T(8,128)S(1)} %bitcast.84) | data formatting | bytes 4456448 | tf_op jit(solution)/shard_map/transpose | solution.py:55
  17.3 6.0 %all-to-all-start = ((f32[8,8,2,34,128]{4,1,3,2,0:T(8,128)}), f32[8,8,2,34,128]{4,1,3,2,0:T(8,128)S(1)}, u32[]{:S(2)}, u32[]{:S(2)}) async-start(f32[8,8,2,34,128]{4,1,3,2,0:T(8,128)} %copy.75), calls=%async_computation | async-start | bytes 4456448 | tf_op jit(solution)/shard_map/all_to_all | solution.py:25
  23.5 0.1 copy.72
  23.6 0.1 copy.71
  23.8 32.0 %all-to-all-done = f32[8,8,2,34,128]{4,1,3,2,0:T(8,128)S(1)} async-done(((f32[8,8,2,34,128]{4,1,3,2,0:T(8,128)}), f32[8,8,2,34,128]{4,1,3,2,0:T(8,128)S(1)}, u32[]{:S(2)}, u32[]{:S(2)}) %all-to-all-start) | async-done | bytes 2228256 | tf_op jit(solution)/shard_map/all_to_all | solution.py:25
  55.8 1.2 copy.76
  57.0 1.2 fusion.11
  58.2 1.2 copy.77
  59.5 10.2 %all-to-all-start.1 = ((f32[16,2,34,128]{3,1,2,0:T(2,128)}), f32[16,2,34,128]{3,1,2,0:T(2,128)S(1)}, u32[]{:S(2)}, u32[]{:S(2)}) async-start(f32[16,2,34,128]{3,1,2,0:T(2,128)} %copy.77), calls=%async_computation.1 | async-start | bytes 1114112 | tf_op jit(solution)/shard_map/all_to_all | solution.py:25
  69.8 17.7 %all-to-all-done.1 = f32[16,2,34,128]{3,1,2,0:T(2,128)S(1)} async-done(((f32[16,2,34,128]{3,1,2,0:T(2,128)}), f32[16,2,34,128]{3,1,2,0:T(2,128)S(1)}, u32[]{:S(2)}, u32[]{:S(2)}) %all-to-all-start.1) | async-done | bytes 557088 | tf_op jit(solution)/shard_map/all_to_all | solution.py:25
  87.5 0.7 convolution_bitcast_fusion
  88.2 1.2 copy.79
  89.4 4.1 %all-to-all-start.2 = ((f32[16,2,34,128]{3,1,2,0:T(2,128)}), f32[16,2,34,128]{3,1,2,0:T(2,128)}, u32[]{:S(2)}, u32[]{:S(2)}) async-start(f32[16,2,34,128]{3,1,2,0:T(2,128)} %copy.79), calls=%async_computation.2 | async-start | bytes 1114112 | tf_op jit(solution)/shard_map/all_to_all | solution.py:25
  93.6 2.7 %collective-permute-start = (f32[2,60,120]{2,0,1:T(2,128)S(1)}, f32[2,60,120]{2,0,1:T(2,128)S(1)}, u32[]{:S(2)}, u32[]{:S(2)}) collective-permute-start(f32[2,60,120]{2,0,1:T(2,128)S(1)} %bitcast.92), channel_id=1, source_target_pairs={{0,1},{1,0},{2,3},{3,2},{4,5},{5,4},{6,7},{7,6},{8,9},{9,8},{10,11... | collective-permute-start | bytes 172808 | tf_op jit(solution)/shard_map/ppermute | solution.py:44
  96.3 0.4 collective-permute-start.1
  96.7 4.0 %collective-permute-done.1 = f32[60]{0:T(128)S(1)} collective-permute-done((f32[60]{0:T(128)S(1)}, f32[60]{0:T(128)S(1)}, u32[]{:S(2)}, u32[]{:S(2)}) %collective-permute-start.1) | collective-permute-done | bytes 272 | tf_op jit(solution)/shard_map/ppermute | solution.py:45
  100.7 0.1 mul.104
  100.9 0.1 copy.81
  101.0 9.5 %all-to-all-done.2 = f32[16,2,34,128]{3,1,2,0:T(2,128)} async-done(((f32[16,2,34,128]{3,1,2,0:T(2,128)}), f32[16,2,34,128]{3,1,2,0:T(2,128)}, u32[]{:S(2)}, u32[]{:S(2)}) %all-to-all-start.2) | async-done | bytes 557088 | tf_op jit(solution)/shard_map/all_to_all | solution.py:25
  110.5 4.0 %all-to-all-start.3 = ((f32[16,2,34,128]{3,1,2,0:T(2,128)}), f32[16,2,34,128]{3,1,2,0:T(2,128)S(1)}, u32[]{:S(2)}, u32[]{:S(2)}) async-start(f32[16,2,34,128]{3,1,2,0:T(2,128)} %all-to-all-done.2), calls=%async_computation.3 | async-start | bytes 1114112 | tf_op jit(solution)/shard_map/all_to_all | solution.py:25
  114.7 11.7 %all-to-all-done.3 = f32[16,2,34,128]{3,1,2,0:T(2,128)S(1)} async-done(((f32[16,2,34,128]{3,1,2,0:T(2,128)}), f32[16,2,34,128]{3,1,2,0:T(2,128)S(1)}, u32[]{:S(2)}, u32[]{:S(2)}) %all-to-all-start.3) | async-done | bytes 557088 | tf_op jit(solution)/shard_map/all_to_all | solution.py:25
  126.4 0.4 reshape.166
  126.8 0.6 reshape.167
  127.5 0.6 convolution_bitcast_fusion.1
  128.0 1.3 collective-permute-start.2
  129.3 0.6 convolution_bitcast_fusion.2
  129.9 8.7 %collective-permute-done.2 = f32[60,2,576]{2,0,1:T(8,128)S(1)} collective-permute-done((f32[60,2,576]{2,0,1:T(8,128)S(1)}, f32[60,2,576]{2,0,1:T(8,128)S(1)}, u32[]{:S(2)}, u32[]{:S(2)}) %collective-permute-start.2) | collective-permute-done | bytes 276512 | tf_op jit(solution)/shard_map/ppermute | solution.py:81
  138.7 1.3 copy.84
  (34 shorter events, 0.9 us)
Async XLA Ops:
  17.3 6.0 %copy-start.1 = (s32[64,3]{0,1:T(4,128)S(1)}, s32[64,3]{0,1:T(4,128)}, u32[]{:S(2)}) copy-start(s32[64,3]{0,1:T(4,128)} %param.8) | copy-start | bytes 2308
  17.3 6.0 %copy-start.2 = (s32[16,3]{0,1:T(4,128)S(1)}, s32[16,3]{0,1:T(4,128)}, u32[]{:S(2)}) copy-start(s32[16,3]{0,1:T(4,128)} %param.10) | copy-start | bytes 580
  17.3 38.5 %all-to-all-start = ((f32[8,8,2,34,128]{4,1,3,2,0:T(8,128)}), f32[8,8,2,34,128]{4,1,3,2,0:T(8,128)S(1)}, u32[]{:S(2)}, u32[]{:S(2)}) async-start(f32[8,8,2,34,128]{4,1,3,2,0:T(8,128)} %copy.75), calls=%async_computation | async-start | bytes 4456448 | tf_op jit(solution)/shard_map/all_to_all | solution.py:25
  57.0 12.7 %copy-start.3 = (s32[16,3]{0,1:T(4,128)S(1)}, s32[16,3]{0,1:T(4,128)}, u32[]{:S(2)}) copy-start(s32[16,3]{0,1:T(4,128)} %param.9) | copy-start | bytes 580
  57.0 12.7 %copy-start.4 = (s32[16,3]{0,1:T(4,128)S(1)}, s32[16,3]{0,1:T(4,128)}, u32[]{:S(2)}) copy-start(s32[16,3]{0,1:T(4,128)} %param.11) | copy-start | bytes 580
  59.5 34.1 %copy-start = (f32[1,2,60,120]{3,1,2,0:T(2,128)S(1)}, f32[1,2,60,120]{3,1,2,0:T(2,128)}, u32[]{:S(2)}) copy-start(f32[1,2,60,120]{3,1,2,0:T(2,128)} %param.12) | copy-start | bytes 172804
  59.5 36.8 %copy-start.5 = (f32[1,60]{1,0:T(1,128)S(1)}, f32[1,60]{1,0:T(1,128)}, u32[]{:S(2)}) copy-start(f32[1,60]{1,0:T(1,128)} %param.13) | copy-start | bytes 724
  59.5 28.0 %all-to-all-start.1 = ((f32[16,2,34,128]{3,1,2,0:T(2,128)}), f32[16,2,34,128]{3,1,2,0:T(2,128)S(1)}, u32[]{:S(2)}, u32[]{:S(2)}) async-start(f32[16,2,34,128]{3,1,2,0:T(2,128)} %copy.77), calls=%async_computation.1 | async-start | bytes 1114112 | tf_op jit(solution)/shard_map/all_to_all | solution.py:25
  89.4 21.1 %all-to-all-start.2 = ((f32[16,2,34,128]{3,1,2,0:T(2,128)}), f32[16,2,34,128]{3,1,2,0:T(2,128)}, u32[]{:S(2)}, u32[]{:S(2)}) async-start(f32[16,2,34,128]{3,1,2,0:T(2,128)} %copy.79), calls=%async_computation.2 | async-start | bytes 1114112 | tf_op jit(solution)/shard_map/all_to_all | solution.py:25
  93.6 7.2 %collective-permute-start = (f32[2,60,120]{2,0,1:T(2,128)S(1)}, f32[2,60,120]{2,0,1:T(2,128)S(1)}, u32[]{:S(2)}, u32[]{:S(2)}) collective-permute-start(f32[2,60,120]{2,0,1:T(2,128)S(1)} %bitcast.92), channel_id=1, source_target_pairs={{0,1},{1,0},{2,3},{3,2},{4,5},{5,4},{6,7},{7,6},{8,9},{9,8},{10,11... | collective-permute-start | bytes 172808 | tf_op jit(solution)/shard_map/ppermute | solution.py:44
  96.3 4.3 %collective-permute-start.1 = (f32[60]{0:T(128)S(1)}, f32[60]{0:T(128)S(1)}, u32[]{:S(2)}, u32[]{:S(2)}) collective-permute-start(f32[60]{0:T(128)S(1)} %get-tuple-element.21), channel_id=1, source_target_pairs={{0,1},{1,0},{2,3},{3,2},{4,5},{5,4},{6,7},{7,6},{8,9},{9,8},{10,11... | collective-permute-start | bytes 728 | tf_op jit(solution)/shard_map/ppermute | solution.py:45
  110.5 15.8 %all-to-all-start.3 = ((f32[16,2,34,128]{3,1,2,0:T(2,128)}), f32[16,2,34,128]{3,1,2,0:T(2,128)S(1)}, u32[]{:S(2)}, u32[]{:S(2)}) async-start(f32[16,2,34,128]{3,1,2,0:T(2,128)} %all-to-all-done.2), calls=%async_computation.3 | async-start | bytes 1114112 | tf_op jit(solution)/shard_map/all_to_all | solution.py:25
  128.0 10.5 %collective-permute-start.2 = (f32[60,2,576]{2,0,1:T(8,128)S(1)}, f32[60,2,576]{2,0,1:T(8,128)S(1)}, u32[]{:S(2)}, u32[]{:S(2)}) collective-permute-start(f32[60,2,576]{2,0,1:T(8,128)S(1)} %convolution_bitcast_fusion.1), channel_id=1, source_target_pairs={{0,1},{1,0},{2,3},{3,2},{4,5},{5,4},{6,7},{7,6},{8,9},{9,8},{10,11... | collective-permute-start | bytes 829448 | tf_op jit(solution)/shard_map/ppermute | solution.py:81

commit v2 on v1

v2 whole, which is shorter than its diff:
```python
import functools

import jax
import jax.numpy as jnp
from jax import lax
from jax.experimental import pallas as pl
from jax.experimental.pallas import tpu as pltpu
from jax.sharding import PartitionSpec as P

KG = 16
HP = lax.Precision.HIGHEST
LANES = 128
HALF = 64


def phases(points, cells):
    turns = jnp.sum(points[:, None, :] * cells[None, :, :], axis=-1) % KG
    angle = turns.astype(jnp.float32) * (2.0 * 3.141592653589793 / KG)
    return jnp.concatenate([jnp.cos(angle), jnp.sin(angle)], axis=0)


def exchange(parts, axis):
    return lax.all_to_all(parts, axis, split_axis=0, concat_axis=0, tiled=True)


def turn(table, block, count):
    both = jnp.dot(table, block, precision=HP, preferred_element_type=jnp.float32)
    parts = []
    for at in range(0, block.shape[1], LANES):
        cos_part = both[:count, at : at + LANES]
        sin_part = pltpu.roll(both[count:, at : at + LANES], HALF, 1)
        lane = lax.broadcasted_iota(jnp.int32, sin_part.shape, 1)
        parts.append(cos_part + jnp.where(lane < HALF, -sin_part, sin_part))
    return parts


def lay_out(x_ref, o_ref, held):
    r = pl.program_id(0)
    count = pl.num_programs(0)
    modes, pairs = x_ref.shape[-2:]

    @pl.when(r == 0)
    def _():
        held[...] = jnp.zeros_like(held)

    held[:modes] = x_ref[0, 0, 0]
    held[HALF : HALF + modes] = x_ref[1, 0, 0]
    o_ref[pl.ds(r, pairs, stride=8), :] = held[...].T


def electron(g_ref, x_ref, o_ref, *, nk, src, span):
    step = pl.program_id(0)
    for m in range(2):
        cols = []
        for p in range(span):
            rows = [x_ref[i * 2 + m, p] for i in range(src)]
            cols.append(jnp.concatenate(rows, axis=0))
        parts = turn(g_ref[...], jnp.concatenate(cols, axis=1), nk)
        total = o_ref.shape[0] // nk
        for p in range(span):
            at = (step * span + p) * 2 + m
            o_ref[pl.ds(at, nk, stride=total), :] = parts[p]


def phonon(g_ref, x_ref, o_ref, *, nq, ns):
    rows = x_ref.shape[0] // ns
    group = 8
    for start in range(0, rows, group):
        cols = [x_ref[pl.ds(start + t, ns, stride=rows), :] for t in range(group)]
        parts = turn(g_ref[...], jnp.concatenate(cols, axis=1), nq)
        for t in range(group):
            o_ref[pl.ds(start + t, nq, stride=rows), :] = parts[t]


def modes_of(x_ref, w_ref, o_ref, *, nk, pts, kk):
    count = nk * pts
    x = jnp.concatenate(
        [x_ref[pl.ds(0, count, stride=2), :], x_ref[pl.ds(1, count, stride=2), :]], axis=1
    )
    res = jnp.dot(x, w_ref[...], precision=HP, preferred_element_type=jnp.float32)
    for k in range(nk):
        for m in range(2):
            base = ((k // kk) * 2 + m) * pts * kk + k % kk
            o_ref[pl.ds(base, pts, stride=kk), :] = res[
                k * pts : (k + 1) * pts, m * LANES : (m + 1) * LANES
            ]


def finish(x_ref, o_ref, *, kk):
    modes, _, _, _, pairs = o_ref.shape
    for k in range(kk):
        turned = x_ref[pl.ds(k, pairs, stride=kk), :].T
        o_ref[:, 0, k, 0, :] = turned[:modes]
        o_ref[:, 0, k, 1, :] = turned[HALF : HALF + modes]


def call(body, out_shape, *args, **kw):
    return pl.pallas_call(
        body, out_shape=jax.ShapeDtypeStruct(out_shape, jnp.float32), **kw
    )(*args)


def shards(
    coupling, electron_cells, phonon_cells, kpoint_index, qpoint_index, eigenvectors, frequencies
):
    re_size = lax.axis_size("re")
    rp_size = lax.axis_size("rp")
    _, nr, _, modes, pairs = coupling.shape
    nk = kpoint_index.shape[0]
    nq = qpoint_index.shape[0]
    ns = phonon_cells.shape[0]
    peers = re_size * 2
    pts = pairs // peers
    kk = nk // re_size

    packed = jnp.concatenate(
        [eigenvectors[0].reshape(2 * modes, -1), jnp.pad(frequencies, ((0, 0), (0, modes)))]
    )
    other = lax.ppermute(packed, "mode", [(0, 1), (1, 0)])
    both = jnp.stack([packed, other])
    both = jnp.where(lax.axis_index("mode") == 0, both, both[::-1])
    scale = lax.rsqrt(2.0 * both[:, -1, :modes]).reshape(-1)
    vec = both[:, :-1].reshape(2, 2, modes, 2 * modes) * scale
    real = jnp.stack([vec[:, 0], -vec[:, 1]], axis=1)
    imag = jnp.stack([vec[:, 1], vec[:, 0]], axis=1)
    weight = jnp.stack([real, imag], axis=3)
    weight = weight.reshape(2, 2, modes, 2, 2, modes).transpose(0, 1, 2, 4, 3, 5)
    gap = HALF - modes
    weight = jnp.pad(weight, ((0, 0), (0, 0), (0, gap), (0, 0), (0, 0), (0, gap)))
    weight = weight.reshape(2 * LANES, 2 * LANES)

    laid = call(
        lay_out,
        (pairs * nr, LANES),
        coupling,
        grid=(nr,),
        in_specs=[pl.BlockSpec((2, 1, 1, modes, pairs), lambda r: (0, r, 0, 0, 0))],
        out_specs=pl.BlockSpec((pairs * nr, LANES), lambda r: (0, 0)),
        scratch_shapes=[pltpu.VMEM((LANES, pairs), jnp.float32)],
    )
    got = exchange(laid.reshape(peers, pts * nr, LANES), ("re", "mode"))
    span = 9
    bloch_k = call(
        functools.partial(electron, nk=nk, src=re_size, span=span),
        (nk * pts * 2, LANES),
        phases(kpoint_index, electron_cells),
        got.reshape(peers, pts, nr, LANES),
        grid=(pts // span,),
        in_specs=[
            pl.BlockSpec((2 * nk, re_size * nr), lambda i: (0, 0)),
            pl.BlockSpec((peers, span, nr, LANES), lambda i: (0, i, 0, 0)),
        ],
        out_specs=pl.BlockSpec((nk * pts * 2, LANES), lambda i: (0, 0)),
    )

    got = exchange(bloch_k.reshape(rp_size, pts * 2, LANES), "rp")
    bloch_kq = call(
        functools.partial(phonon, nq=nq, ns=ns),
        (nq * pts * 2, LANES),
        phases(qpoint_index, phonon_cells),
        got.reshape(ns * pts * 2, LANES),
    )

    got = exchange(bloch_kq.reshape(rp_size, pts * 2, LANES), "rp")
    rotated = call(
        functools.partial(modes_of, nk=nk, pts=pts, kk=kk),
        (peers * pts * kk, LANES),
        got.reshape(nk * pts * 2, LANES),
        weight,
    )

    got = exchange(rotated.reshape(peers, pts * kk, LANES), ("re", "mode"))
    return call(
        functools.partial(finish, kk=kk),
        (modes, 1, kk, 2, pairs),
        got.reshape(pairs * kk, LANES),
    )


def solution(mesh):
    placed = (
        P(None, "re", "rp", "mode", None),
        P(),
        P(),
        P(),
        P(),
        P("rp", None, "mode", None),
        P("rp", "mode"),
    )
    return jax.shard_map(
        shards,
        mesh=mesh,
        in_specs=placed,
        out_specs=P("mode", "rp", "re", None, None),
        check_vma=False,
    )
```

time: 141 us -> 137 us (0.972)
  Pallas kernels: 0 us -> 18.4 us
  waiting for transfers between devices: 83.6 us -> 65.6 us
  blocking collectives: 0 us -> 17.7 us
  local copies, waits for them, and re-layouts: 16.3 us -> 9.04 us
  other arithmetic: 8.23 us -> 1.99 us
  starting transfers between devices: 28.7 us -> 23.6 us
  matrix products: 3.03 us -> 0 us
    pallas_call x0 -> x5, Pallas kernels: none -> 18.4 us  [call(): pl.pallas_call(body, out_shape=jax.ShapeDtypeStruct(out_shape, jnp.float3...]
    all_to_all x0 -> x1, blocking collectives: none -> 17.7 us  [exchange(): return lax.all_to_all(parts, axis, split_axis=0, concat_axis=0, tiled=True)]
    ppermute x3 -> x1, waiting for transfers between devices: 12.6 us -> 0.01 us  [shards(): other = lax.ppermute(packed, 'mode', [(0, 1), (1, 0)])]
    unnamed x1 -> x0, other arithmetic: 7.6 us -> none
    unnamed x12 -> x21, local copies, waits for them, and re-layouts: 0.03 us -> 6.94 us
    all_to_all x4 -> x3, waiting for transfers between devices: 70.9 us -> 65.6 us  [exchange(): return lax.all_to_all(parts, axis, split_axis=0, concat_axis=0, tiled=True)]
    reshape x6 -> x1, local copies, waits for them, and re-layouts: 5.06 us -> 1.16 us  [shards(): weight = weight.reshape(2 * LANES, 2 * LANES)]
    ppermute x3 -> x1, starting transfers between devices: 4.34 us -> 0.69 us  [shards(): other = lax.ppermute(packed, 'mode', [(0, 1), (1, 0)])]
  transfers between devices with their start and end apart: 7 -> 4, of which waited for: 6 -> 3; matrix products, arithmetic and copies ran while one was open for 1% -> 3% of each run, Pallas kernels for 0% -> 2%
where the time goes in v2:
time: 137 us
  waiting for transfers between devices  65.6 us (48%)
  starting transfers between devices  23.6 us (17%)
  Pallas kernels  18.4 us (13%)
  blocking collectives  17.7 us (13%)
  local copies, waits for them, and re-layouts  9.04 us (7%)
  other arithmetic  1.99 us (1%)
    all_to_all x3, waiting for transfers between devices, exchange(): return lax.all_to_all(parts, axis, split_axis=0, concat_axis=0, tiled=True)  65.6 us
    all_to_all x3, starting transfers between devices, exchange(): return lax.all_to_all(parts, axis, split_axis=0, concat_axis=0, tiled=True)  22.9 us
    pallas_call x5, Pallas kernels, call(): pl.pallas_call(body, out_shape=jax.ShapeDtypeStruct(out_shape, jnp.float3...  18.4 us
    all_to_all x1, blocking collectives, exchange(): return lax.all_to_all(parts, axis, split_axis=0, concat_axis=0, tiled=True)  17.7 us
    unnamed x21, local copies, waits for them, and re-layouts  6.94 us
  transfers between devices with their start and end apart: 4, of which 3 were waited for; matrix products, arithmetic and copies ran while one was open for 3% of the time, Pallas kernels for 2%

profile of v2, /device:TPU:1, one launch (start us, length us, event | category | flops | bytes accessed | tf_op | source)
XLA Modules:
  0.0 136.6 jit_solution(3176162545389446057)
XLA Ops:
  0.0 3.5 %copy.38.x_ref = f32[2,8,1,60,576]{4,3,2,1,0:T(8,128)} copy(f32[2,8,1,60,576]{4,2,3,1,0:T(1,128)} %param.7) | data formatting | bytes 4423680 | tf_op args[0]
  3.5 6.2 %shard_map.73 = f32[4608,128]{1,0:T(8,128)} custom-call(f32[2,8,1,60,576]{4,3,2,1,0:T(8,128)} %copy.38.x_ref), custom_call_target="tpu_custom_call" | custom-call | tf_op jit(solution)/shard_map/pallas_call | solution.py:98
  9.7 7.7 %all-to-all-start = ((f32[16,288,128]{2,1,0:T(8,128)}), f32[16,288,128]{2,1,0:T(8,128)S(1)}, u32[]{:S(2)}, u32[]{:S(2)}) async-start(f32[16,288,128]{2,1,0:T(8,128)} %bitcast.19), calls=%async_computation | async-start | bytes 4718592 | tf_op jit(solution)/shard_map/all_to_all | solution.py:23
  17.5 0.1 multiply_reduce_fusion
  17.6 0.6 pad_maximum_fusion.4.g_ref
  18.2 33.5 %all-to-all-done = f32[16,288,128]{2,1,0:T(8,128)S(1)} async-done(((f32[16,288,128]{2,1,0:T(8,128)}), f32[16,288,128]{2,1,0:T(8,128)S(1)}, u32[]{:S(2)}, u32[]{:S(2)}) %all-to-all-start) | async-done | bytes 2359328 | tf_op jit(solution)/shard_map/all_to_all | solution.py:23
  51.7 1.4 %copy-done = f32[16,288,128]{2,1,0:T(8,128)} copy-done((f32[16,288,128]{2,1,0:T(8,128)}, f32[16,288,128]{2,1,0:T(8,128)S(1)}, u32[]{:S(2)}) %copy-start) | copy-done | bytes 2359320
  53.2 4.4 %shard_map.74 = f32[1152,128]{1,0:T(8,128)} custom-call(f32[32,64]{1,0:T(8,128)} %pad_maximum_fusion.4.g_ref, f32[16,36,8,128]{3,2,1,0:T(8,128)} %bitcast.18), custom_call_target="tpu_custom_call" | custom-call | tf_op jit(solution)/shard_map/pallas_call | solution.py:98
  57.6 11.7 %all-to-all-start.1 = ((f32[16,72,128]{2,1,0:T(8,128)}), f32[16,72,128]{2,1,0:T(8,128)S(1)}, u32[]{:S(2)}, u32[]{:S(2)}) async-start(f32[16,72,128]{2,1,0:T(8,128)} %bitcast.25), calls=%async_computation.1 | async-start | bytes 1179648 | tf_op jit(solution)/shard_map/all_to_all | solution.py:23
  69.3 0.7 collective-permute-start
  70.0 0.1 multiply_reduce_fusion.1
  70.2 0.6 pad_maximum_fusion.3.g_ref
  70.8 17.0 %all-to-all-done.1 = f32[16,72,128]{2,1,0:T(8,128)S(1)} async-done(((f32[16,72,128]{2,1,0:T(8,128)}), f32[16,72,128]{2,1,0:T(8,128)S(1)}, u32[]{:S(2)}, u32[]{:S(2)}) %all-to-all-start.1) | async-done | bytes 589856 | tf_op jit(solution)/shard_map/all_to_all | solution.py:23
  87.8 0.8 copy-done.2
  88.6 3.0 %shard_map.75 = f32[1152,128]{1,0:T(8,128)} custom-call(f32[32,16]{1,0:T(8,128)} %pad_maximum_fusion.3.g_ref, f32[1152,128]{1,0:T(8,128)} %bitcast.22), custom_call_target="tpu_custom_call" | custom-call | tf_op jit(solution)/shard_map/pallas_call | solution.py:98
  91.6 3.5 %all-to-all-start.2 = ((f32[16,72,128]{2,1,0:T(8,128)}), f32[16,72,128]{2,1,0:T(8,128)S(1)}, u32[]{:S(2)}, u32[]{:S(2)}) async-start(f32[16,72,128]{2,1,0:T(8,128)} %bitcast.21), calls=%async_computation.2 | async-start | bytes 1179648 | tf_op jit(solution)/shard_map/all_to_all | solution.py:23
  95.2 0.1 copy.42
  95.3 0.1 rsqrt.11
  95.5 0.1 pad_maximum_fusion.1
  95.6 0.1 copy.44
  95.7 0.2 stack.31
  95.9 0.1 copy.43
  96.0 0.2 stack.29
  96.2 0.3 maximum_bitcast_fusion
  96.5 0.4 copy.47
  96.9 0.2 pad.9.clone
  97.1 1.2 reshape.55.w_ref
  98.2 15.1 %all-to-all-done.2 = f32[16,72,128]{2,1,0:T(8,128)S(1)} async-done(((f32[16,72,128]{2,1,0:T(8,128)}), f32[16,72,128]{2,1,0:T(8,128)S(1)}, u32[]{:S(2)}, u32[]{:S(2)}) %all-to-all-start.2) | async-done | bytes 589856 | tf_op jit(solution)/shard_map/all_to_all | solution.py:23
  113.3 0.8 copy-done.1
  114.1 2.6 %shard_map.76 = f32[1152,128]{1,0:T(8,128)} custom-call(f32[1152,128]{1,0:T(8,128)} %bitcast.20, f32[256,256]{1,0:T(8,128)} %reshape.55.w_ref), custom_call_target="tpu_custom_call" | custom-call | tf_op jit(solution)/shard_map/pallas_call | solution.py:98
  116.7 17.7 %all_to_all.20 = f32[16,72,128]{2,1,0:T(8,128)} all-to-all(f32[16,72,128]{2,1,0:T(8,128)} %bitcast.23), channel_id=1, replica_groups=mesh['re'=8,'rp'=16,'mode'=2] {'re','mode'}, dimensions={0} | all-to-all | bytes 1179648 | tf_op jit(solution)/shard_map/all_to_all | solution.py:23
  134.4 2.2 %shard_map.77 = f32[60,1,2,2,576]{4,3,2,1,0:T(2,128)} custom-call(f32[1152,128]{1,0:T(8,128)} %bitcast.24), custom_call_target="tpu_custom_call" | custom-call | tf_op jit(solution)/shard_map/pallas_call | solution.py:98
  (27 shorter events, 0.3 us)
Async XLA Ops:
  9.7 7.7 %copy-start.4 = (s32[64,3]{0,1:T(4,128)S(1)}, s32[64,3]{0,1:T(4,128)}, u32[]{:S(2)}) copy-start(s32[64,3]{0,1:T(4,128)} %param.8) | copy-start | bytes 2308
  9.7 7.7 %copy-start.5 = (s32[16,3]{0,1:T(4,128)S(1)}, s32[16,3]{0,1:T(4,128)}, u32[]{:S(2)}) copy-start(s32[16,3]{0,1:T(4,128)} %param.10) | copy-start | bytes 580
  9.7 42.0 %all-to-all-start = ((f32[16,288,128]{2,1,0:T(8,128)}), f32[16,288,128]{2,1,0:T(8,128)S(1)}, u32[]{:S(2)}, u32[]{:S(2)}) async-start(f32[16,288,128]{2,1,0:T(8,128)} %bitcast.19), calls=%async_computation | async-start | bytes 4718592 | tf_op jit(solution)/shard_map/all_to_all | solution.py:23
  17.4 51.8 %copy-start.3 = (f32[1,2,60,120]{3,1,2,0:T(2,128)S(1)}, f32[1,2,60,120]{3,1,2,0:T(2,128)}, u32[]{:S(2)}) copy-start(f32[1,2,60,120]{3,1,2,0:T(2,128)} %param.12) | copy-start | bytes 172804
  17.4 51.9 %copy-start.8 = (f32[1,60]{1,0:T(1,128)S(1)}, f32[1,60]{1,0:T(1,128)}, u32[]{:S(2)}) copy-start(f32[1,60]{1,0:T(1,128)} %param.13) | copy-start | bytes 724
  17.5 52.6 %copy-start.6 = (s32[16,3]{0,1:T(4,128)S(1)}, s32[16,3]{0,1:T(4,128)}, u32[]{:S(2)}) copy-start(s32[16,3]{0,1:T(4,128)} %param.9) | copy-start | bytes 580
  17.5 52.6 %copy-start.7 = (s32[16,3]{0,1:T(4,128)S(1)}, s32[16,3]{0,1:T(4,128)}, u32[]{:S(2)}) copy-start(s32[16,3]{0,1:T(4,128)} %param.11) | copy-start | bytes 580
  51.7 1.4 %copy-start = (f32[16,288,128]{2,1,0:T(8,128)}, f32[16,288,128]{2,1,0:T(8,128)S(1)}, u32[]{:S(2)}) copy-start(f32[16,288,128]{2,1,0:T(8,128)S(1)} %all-to-all-done) | copy-start | bytes 7077892
  57.6 30.2 %all-to-all-start.1 = ((f32[16,72,128]{2,1,0:T(8,128)}), f32[16,72,128]{2,1,0:T(8,128)S(1)}, u32[]{:S(2)}, u32[]{:S(2)}) async-start(f32[16,72,128]{2,1,0:T(8,128)} %bitcast.25), calls=%async_computation.1 | async-start | bytes 1179648 | tf_op jit(solution)/shard_map/all_to_all | solution.py:23
  69.3 25.8 %collective-permute-start = (f32[121,120]{1,0:T(8,128)S(1)}, f32[121,120]{1,0:T(8,128)S(1)}, u32[]{:S(2)}, u32[]{:S(2)}) collective-permute-start(f32[121,120]{1,0:T(8,128)S(1)} %get-tuple-element.9), channel_id=1, source_target_pairs={{0,1},{1,0},{2,3},{3,2},{4,5},{5,4},{6,7},{7,6},{8,9},{9,8},{10,11... | collective-permute-start | bytes 174248 | tf_op jit(solution)/shard_map/ppermute | solution.py:119
  87.8 0.8 copy-start.2
  91.6 21.6 %all-to-all-start.2 = ((f32[16,72,128]{2,1,0:T(8,128)}), f32[16,72,128]{2,1,0:T(8,128)S(1)}, u32[]{:S(2)}, u32[]{:S(2)}) async-start(f32[16,72,128]{2,1,0:T(8,128)} %bitcast.21), calls=%async_computation.2 | async-start | bytes 1179648 | tf_op jit(solution)/shard_map/all_to_all | solution.py:23
  113.3 0.8 copy-start.1

commit v3 on v2

--- a/solution.py
+++ b/solution.py
@@ -37,29 +37,27 @@
 def lay_out(x_ref, o_ref, held):
     r = pl.program_id(0)
     count = pl.num_programs(0)
-    modes, pairs = x_ref.shape[-2:]
+    modes, _, pairs = x_ref.shape[-3:]
 
     @pl.when(r == 0)
     def _():
         held[...] = jnp.zeros_like(held)
 
-    held[:modes] = x_ref[0, 0, 0]
-    held[HALF : HALF + modes] = x_ref[1, 0, 0]
+    held[:modes] = x_ref[0, 0, :, 0, :]
+    held[HALF : HALF + modes] = x_ref[1, 0, :, 0, :]
     o_ref[pl.ds(r, pairs, stride=8), :] = held[...].T
 
 
-def electron(g_ref, x_ref, o_ref, *, nk, src, span):
-    step = pl.program_id(0)
-    for m in range(2):
+def electron(g_ref, x_ref, o_ref, *, nk, src):
+    points = o_ref.shape[0] // nk
+    group = 8
+    for start in range(0, points, group):
         cols = []
-        for p in range(span):
-            rows = [x_ref[i * 2 + m, p] for i in range(src)]
-            cols.append(jnp.concatenate(rows, axis=0))
+        for p in range(start, start + group):
+            cols.append(jnp.concatenate([x_ref[i, p] for i in range(src)], axis=0))
         parts = turn(g_ref[...], jnp.concatenate(cols, axis=1), nk)
-        total = o_ref.shape[0] // nk
-        for p in range(span):
-            at = (step * span + p) * 2 + m
-            o_ref[pl.ds(at, nk, stride=total), :] = parts[p]
+        for t in range(group):
+            o_ref[pl.ds(start + t, nk, stride=points), :] = parts[t]
 
 
 def phonon(g_ref, x_ref, o_ref, *, nq, ns):
@@ -73,17 +71,15 @@
 
 
 def modes_of(x_ref, w_ref, o_ref, *, nk, pts, kk):
-    count = nk * pts
-    x = jnp.concatenate(
-        [x_ref[pl.ds(0, count, stride=2), :], x_ref[pl.ds(1, count, stride=2), :]], axis=1
-    )
-    res = jnp.dot(x, w_ref[...], precision=HP, preferred_element_type=jnp.float32)
     for k in range(nk):
+        at = 2 * k * pts
+        x = jnp.concatenate(
+            [x_ref[at : at + pts, :], x_ref[at + pts : at + 2 * pts, :]], axis=1
+        )
+        res = jnp.dot(x, w_ref[...], precision=HP, preferred_element_type=jnp.float32)
         for m in range(2):
             base = ((k // kk) * 2 + m) * pts * kk + k % kk
-            o_ref[pl.ds(base, pts, stride=kk), :] = res[
-                k * pts : (k + 1) * pts, m * LANES : (m + 1) * LANES
-            ]
+            o_ref[pl.ds(base, pts, stride=kk), :] = res[:, m * LANES : (m + 1) * LANES]
 
 
 def finish(x_ref, o_ref, *, kk):
@@ -94,10 +90,15 @@
         o_ref[:, 0, k, 1, :] = turned[HALF : HALF + modes]
 
 
+WHOLE = pl.BlockSpec(memory_space=pltpu.VMEM)
+
+
+def near(x):
+    return pltpu.with_memory_space_constraint(x, pltpu.VMEM)
+
+
 def call(body, out_shape, *args, **kw):
-    return pl.pallas_call(
-        body, out_shape=jax.ShapeDtypeStruct(out_shape, jnp.float32), **kw
-    )(*args)
+    return pl.pallas_call(body, out_shape=pltpu.VMEM(out_shape, jnp.float32), **kw)(*args)
 
 
 def shards(
@@ -132,25 +133,20 @@
     laid = call(
         lay_out,
         (pairs * nr, LANES),
-        coupling,
+        coupling.transpose(0, 1, 3, 2, 4),
         grid=(nr,),
-        in_specs=[pl.BlockSpec((2, 1, 1, modes, pairs), lambda r: (0, r, 0, 0, 0))],
+        in_specs=[pl.BlockSpec((2, 1, modes, 1, pairs), lambda r: (0, r, 0, 0, 0))],
         out_specs=pl.BlockSpec((pairs * nr, LANES), lambda r: (0, 0)),
         scratch_shapes=[pltpu.VMEM((LANES, pairs), jnp.float32)],
     )
-    got = exchange(laid.reshape(peers, pts * nr, LANES), ("re", "mode"))
-    span = 9
+    got = exchange(laid.reshape(re_size, 2 * pts * nr, LANES), "re")
     bloch_k = call(
-        functools.partial(electron, nk=nk, src=re_size, span=span),
+        functools.partial(electron, nk=nk, src=re_size),
         (nk * pts * 2, LANES),
         phases(kpoint_index, electron_cells),
-        got.reshape(peers, pts, nr, LANES),
-        grid=(pts // span,),
-        in_specs=[
-            pl.BlockSpec((2 * nk, re_size * nr), lambda i: (0, 0)),
-            pl.BlockSpec((peers, span, nr, LANES), lambda i: (0, i, 0, 0)),
-        ],
-        out_specs=pl.BlockSpec((nk * pts * 2, LANES), lambda i: (0, 0)),
+        near(got.reshape(re_size, 2 * pts, nr, LANES)),
+        in_specs=[WHOLE, WHOLE],
+        out_specs=WHOLE,
     )
 
     got = exchange(bloch_k.reshape(rp_size, pts * 2, LANES), "rp")
@@ -158,23 +154,28 @@
         functools.partial(phonon, nq=nq, ns=ns),
         (nq * pts * 2, LANES),
         phases(qpoint_index, phonon_cells),
-        got.reshape(ns * pts * 2, LANES),
+        near(got.reshape(ns * pts * 2, LANES)),
+        in_specs=[WHOLE, WHOLE],
+        out_specs=WHOLE,
     )
 
-    got = exchange(bloch_kq.reshape(rp_size, pts * 2, LANES), "rp")
+    got = exchange(bloch_kq.reshape(rp_size * 2, pts // 4, 4, LANES), ("rp", "mode"))
     rotated = call(
         functools.partial(modes_of, nk=nk, pts=pts, kk=kk),
         (peers * pts * kk, LANES),
-        got.reshape(nk * pts * 2, LANES),
+        near(got.reshape(nk * pts * 2, LANES)),
         weight,
+        in_specs=[WHOLE, WHOLE],
+        out_specs=WHOLE,
     )
 
     got = exchange(rotated.reshape(peers, pts * kk, LANES), ("re", "mode"))
-    return call(
+    return pl.pallas_call(
         functools.partial(finish, kk=kk),
-        (modes, 1, kk, 2, pairs),
-        got.reshape(pairs * kk, LANES),
-    )
+        out_shape=jax.ShapeDtypeStruct((modes, 1, kk, 2, pairs), jnp.float32),
+        in_specs=[WHOLE],
+        out_specs=WHOLE,
+    )(near(got.reshape(pairs * kk, LANES)))
 
 
 def solution(mesh):

time: 137 us -> 125 us (0.912)
  local copies, waits for them, and re-layouts: 9.04 us -> 3.92 us
  Pallas kernels: 18.4 us -> 14.5 us
  blocking collectives: 17.7 us -> 15.6 us
  waiting for transfers between devices: 65.6 us -> 63.6 us
    unnamed x21 -> x16, local copies, waits for them, and re-layouts: 6.94 us -> 1.82 us
    pallas_call x5, Pallas kernels: 18.4 us -> 14.5 us  [the longest x4 13.4 us: call(): pl.pallas_call(body, out_shape=pltpu.VMEM(out_shape, jnp.float32), **kw)]
    all_to_all x1, blocking collectives: 17.7 us -> 15.6 us  [exchange(): return lax.all_to_all(parts, axis, split_axis=0, concat_axis=0, tiled=True)]
    ppermute x1, starting transfers between devices: 0.69 us -> 2.71 us  [shards(): other = lax.ppermute(packed, 'mode', [(0, 1), (1, 0)])]
    all_to_all x3, waiting for transfers between devices: 65.6 us -> 63.6 us  [exchange(): return lax.all_to_all(parts, axis, split_axis=0, concat_axis=0, tiled=True)]
  transfers between devices with their start and end apart: 4 -> 4, of which waited for: 3 -> 3; matrix products, arithmetic and copies ran while one was open for 3% -> 4% of each run, Pallas kernels for 2% -> 2%
where the time goes in v3:
time: 125 us; the launch traced here: 124 us
  waiting for transfers between devices  63.6 us (51%)
  starting transfers between devices  24.3 us (19%)
  blocking collectives  15.6 us (12%)
  Pallas kernels  14.5 us (12%)
  local copies, waits for them, and re-layouts  3.92 us (3%)
  other arithmetic  2.01 us (2%)
    all_to_all x3, waiting for transfers between devices, exchange(): return lax.all_to_all(parts, axis, split_axis=0, concat_axis=0, tiled=True)  63.6 us
    all_to_all x3, starting transfers between devices, exchange(): return lax.all_to_all(parts, axis, split_axis=0, concat_axis=0, tiled=True)  21.6 us
    all_to_all x1, blocking collectives, exchange(): return lax.all_to_all(parts, axis, split_axis=0, concat_axis=0, tiled=True)  15.6 us
    pallas_call x4, Pallas kernels, call(): pl.pallas_call(body, out_shape=pltpu.VMEM(out_shape, jnp.float32), **kw)  13.4 us
    ppermute x1, starting transfers between devices, shards(): other = lax.ppermute(packed, 'mode', [(0, 1), (1, 0)])  2.71 us
  transfers between devices with their start and end apart: 4, of which 3 were waited for; matrix products, arithmetic and copies ran while one was open for 4% of the time, Pallas kernels for 2%

profile of v3, /device:TPU:1, one launch (start us, length us, event | category | flops | bytes accessed | tf_op | source)
XLA Modules:
  0.0 124.2 jit_solution(17756827186258568092)
XLA Ops:
  0.0 4.9 %shard_map.73 = f32[4608,128]{1,0:T(8,128)S(1)} custom-call(f32[2,8,60,1,576]{4,3,2,1,0:T(1,128)} %bitcast.25), custom_call_target="tpu_custom_call" | custom-call | tf_op jit(solution)/shard_map/pallas_call | solution.py:101
  4.9 1.4 %copy-done = f32[4608,128]{1,0:T(8,128)} copy-done((f32[4608,128]{1,0:T(8,128)}, f32[4608,128]{1,0:T(8,128)S(1)}, u32[]{:S(2)}) %copy-start) | copy-done | bytes 2359320
  6.3 6.0 %all-to-all-start = ((f32[8,576,128]{2,1,0:T(8,128)}), f32[8,576,128]{2,1,0:T(8,128)S(1)}, u32[]{:S(2)}, u32[]{:S(2)}) async-start(f32[8,576,128]{2,1,0:T(8,128)} %bitcast.20), calls=%async_computation | async-start | bytes 4718592 | tf_op jit(solution)/shard_map/all_to_all | solution.py:23
  12.3 0.0 copy-start.1
  12.3 0.1 multiply_reduce_fusion
  12.4 0.1 fusion.7
  12.5 0.6 pad_maximum_fusion.4.g_ref
  13.1 33.5 %all-to-all-done = f32[8,576,128]{2,1,0:T(8,128)S(1)} async-done(((f32[8,576,128]{2,1,0:T(8,128)}), f32[8,576,128]{2,1,0:T(8,128)S(1)}, u32[]{:S(2)}, u32[]{:S(2)}) %all-to-all-start) | async-done | bytes 2359328 | tf_op jit(solution)/shard_map/all_to_all | solution.py:23
  46.6 2.7 %shard_map.74 = f32[1152,128]{1,0:T(8,128)} custom-call(f32[32,64]{1,0:T(8,128)} %pad_maximum_fusion.4.g_ref, f32[8,72,8,128]{3,2,1,0:T(8,128)S(1)} %bitcast.19), custom_call_target="tpu_custom_call" | custom-call | tf_op jit(solution)/shard_map/pallas_call | solution.py:101
  49.3 10.0 %all-to-all-start.1 = ((f32[16,72,128]{2,1,0:T(8,128)}), f32[16,72,128]{2,1,0:T(8,128)S(1)}, u32[]{:S(2)}, u32[]{:S(2)}) async-start(f32[16,72,128]{2,1,0:T(8,128)} %bitcast.3), calls=%async_computation.1 | async-start | bytes 1179648 | tf_op jit(solution)/shard_map/all_to_all | solution.py:23
  59.4 2.7 %collective-permute-start = (f32[121,120]{1,0:T(8,128)S(1)}, f32[121,120]{1,0:T(8,128)S(1)}, u32[]{:S(2)}, u32[]{:S(2)}) collective-permute-start(f32[121,120]{1,0:T(8,128)S(1)} %get-tuple-element.9), channel_id=1, source_target_pairs={{0,1},{1,0},{2,3},{3,2},{4,5},{5,4},{6,7},{7,6},{8,9},{9,8},{10,11... | collective-permute-start | bytes 174248 | tf_op jit(solution)/shard_map/ppermute | solution.py:120
  62.1 0.1 multiply_reduce_fusion.1
  62.2 0.1 fusion.9
  62.3 0.6 pad_maximum_fusion.3.g_ref
  62.9 15.0 %all-to-all-done.1 = f32[16,72,128]{2,1,0:T(8,128)S(1)} async-done(((f32[16,72,128]{2,1,0:T(8,128)}), f32[16,72,128]{2,1,0:T(8,128)S(1)}, u32[]{:S(2)}, u32[]{:S(2)}) %all-to-all-start.1) | async-done | bytes 589856 | tf_op jit(solution)/shard_map/all_to_all | solution.py:23
  77.9 2.7 %shard_map.75 = f32[1152,128]{1,0:T(8,128)} custom-call(f32[32,16]{1,0:T(8,128)} %pad_maximum_fusion.3.g_ref, f32[1152,128]{1,0:T(8,128)S(1)} %bitcast.22), custom_call_target="tpu_custom_call" | custom-call | tf_op jit(solution)/shard_map/pallas_call | solution.py:101
  80.5 5.5 %all-to-all-start.2 = ((f32[32,9,4,128]{3,2,1,0:T(4,128)}), f32[32,9,4,128]{3,2,1,0:T(4,128)S(1)}, u32[]{:S(2)}, u32[]{:S(2)}) async-start(f32[32,9,4,128]{3,2,1,0:T(4,128)} %bitcast.5), calls=%async_computation.2 | async-start | bytes 1179648 | tf_op jit(solution)/shard_map/all_to_all | solution.py:23
  86.2 0.1 copy.38
  86.3 0.1 rsqrt.11
  86.4 0.1 pad_maximum_fusion.1
  86.6 0.1 copy.40
  86.6 0.2 stack.31
  86.9 0.1 copy.39
  86.9 0.2 stack.29
  87.2 0.3 maximum_bitcast_fusion
  87.4 0.4 copy.43
  87.8 0.2 pad.9.clone
  88.0 1.2 reshape.55.w_ref
  89.2 15.1 %all-to-all-done.2 = f32[32,9,4,128]{3,2,1,0:T(4,128)S(1)} async-done(((f32[32,9,4,128]{3,2,1,0:T(4,128)}), f32[32,9,4,128]{3,2,1,0:T(4,128)S(1)}, u32[]{:S(2)}, u32[]{:S(2)}) %all-to-all-start.2) | async-done | bytes 589856 | tf_op jit(solution)/shard_map/all_to_all | solution.py:23
  104.3 3.1 %shard_map.76 = f32[1152,128]{1,0:T(8,128)S(1)} custom-call(f32[1152,128]{1,0:T(8,128)S(1)} %bitcast.21, f32[256,256]{1,0:T(8,128)} %reshape.55.w_ref), custom_call_target="tpu_custom_call" | custom-call | tf_op jit(solution)/shard_map/pallas_call | solution.py:101
  107.4 15.6 %all_to_all.20 = f32[16,72,128]{2,1,0:T(8,128)S(1)} all-to-all(f32[16,72,128]{2,1,0:T(8,128)S(1)} %bitcast.23), channel_id=1, replica_groups=mesh['re'=8,'rp'=16,'mode'=2] {'re','mode'}, dimensions={0} | all-to-all | bytes 1179648 | tf_op jit(solution)/shard_map/all_to_all | solution.py:23
  123.1 1.1 shard_map.77
  (22 shorter events, 0.2 us)
Async XLA Ops:
  4.9 1.4 %copy-start = (f32[4608,128]{1,0:T(8,128)}, f32[4608,128]{1,0:T(8,128)S(1)}, u32[]{:S(2)}) copy-start(f32[4608,128]{1,0:T(8,128)S(1)} %shard_map.73) | copy-start | bytes 7077892
  6.3 6.0 %copy-start.2 = (s32[64,3]{0,1:T(4,128)S(1)}, s32[64,3]{0,1:T(4,128)}, u32[]{:S(2)}) copy-start(s32[64,3]{0,1:T(4,128)} %param.8) | copy-start | bytes 2308
  6.3 6.0 %copy-start.3 = (s32[16,3]{0,1:T(4,128)S(1)}, s32[16,3]{0,1:T(4,128)}, u32[]{:S(2)}) copy-start(s32[16,3]{0,1:T(4,128)} %param.10) | copy-start | bytes 580
  6.3 40.3 %all-to-all-start = ((f32[8,576,128]{2,1,0:T(8,128)}), f32[8,576,128]{2,1,0:T(8,128)S(1)}, u32[]{:S(2)}, u32[]{:S(2)}) async-start(f32[8,576,128]{2,1,0:T(8,128)} %bitcast.20), calls=%async_computation | async-start | bytes 4718592 | tf_op jit(solution)/shard_map/all_to_all | solution.py:23
  12.3 47.1 %copy-start.1 = (f32[1,2,60,120]{3,1,2,0:T(2,128)S(1)}, f32[1,2,60,120]{3,1,2,0:T(2,128)}, u32[]{:S(2)}) copy-start(f32[1,2,60,120]{3,1,2,0:T(2,128)} %param.12) | copy-start | bytes 172804
  12.3 47.1 %copy-start.6 = (f32[1,60]{1,0:T(1,128)S(1)}, f32[1,60]{1,0:T(1,128)}, u32[]{:S(2)}) copy-start(f32[1,60]{1,0:T(1,128)} %param.13) | copy-start | bytes 724
  12.3 49.8 %copy-start.4 = (s32[16,3]{0,1:T(4,128)S(1)}, s32[16,3]{0,1:T(4,128)}, u32[]{:S(2)}) copy-start(s32[16,3]{0,1:T(4,128)} %param.9) | copy-start | bytes 580
  12.3 49.8 %copy-start.5 = (s32[16,3]{0,1:T(4,128)S(1)}, s32[16,3]{0,1:T(4,128)}, u32[]{:S(2)}) copy-start(s32[16,3]{0,1:T(4,128)} %param.11) | copy-start | bytes 580
  49.3 28.6 %all-to-all-start.1 = ((f32[16,72,128]{2,1,0:T(8,128)}), f32[16,72,128]{2,1,0:T(8,128)S(1)}, u32[]{:S(2)}, u32[]{:S(2)}) async-start(f32[16,72,128]{2,1,0:T(8,128)} %bitcast.3), calls=%async_computation.1 | async-start | bytes 1179648 | tf_op jit(solution)/shard_map/all_to_all | solution.py:23
  59.4 26.7 %collective-permute-start = (f32[121,120]{1,0:T(8,128)S(1)}, f32[121,120]{1,0:T(8,128)S(1)}, u32[]{:S(2)}, u32[]{:S(2)}) collective-permute-start(f32[121,120]{1,0:T(8,128)S(1)} %get-tuple-element.9), channel_id=1, source_target_pairs={{0,1},{1,0},{2,3},{3,2},{4,5},{5,4},{6,7},{7,6},{8,9},{9,8},{10,11... | collective-permute-start | bytes 174248 | tf_op jit(solution)/shard_map/ppermute | solution.py:120
  80.5 23.8 %all-to-all-start.2 = ((f32[32,9,4,128]{3,2,1,0:T(4,128)}), f32[32,9,4,128]{3,2,1,0:T(4,128)S(1)}, u32[]{:S(2)}, u32[]{:S(2)}) async-start(f32[32,9,4,128]{3,2,1,0:T(4,128)} %bitcast.5), calls=%async_computation.2 | async-start | bytes 1179648 | tf_op jit(solution)/shard_map/all_to_all | solution.py:23

commit v4 on v3

v4 whole, which is shorter than its diff:
```python
import functools

import jax
import jax.numpy as jnp
from jax import lax
from jax.experimental import pallas as pl
from jax.experimental.pallas import tpu as pltpu
from jax.sharding import PartitionSpec as P

KG = 16
LANES = 128
HALF = 64


def exchange(parts, axis):
    return lax.all_to_all(parts, axis, split_axis=0, concat_axis=0, tiled=True)


def split(x):
    high = x.astype(jnp.bfloat16)
    return high, (x - high.astype(jnp.float32)).astype(jnp.bfloat16)


def dot(a, b):
    return jnp.dot(a, b, preferred_element_type=jnp.float32)


def phases(points_ref, cells_ref, stride=1):
    points = points_ref[...].astype(jnp.float32)
    count = points.shape[1]
    if stride > 1:
        old = lax.broadcasted_iota(jnp.int32, (count, count), 0)
        new = lax.broadcasted_iota(jnp.int32, (count, count), 1)
        at = old % stride * (count // stride) + old // stride
        points = jnp.dot(
            points, jnp.where(at == new, 1.0, 0.0), precision=lax.Precision.HIGHEST
        )
    exact = lax.dot_general(
        points,
        cells_ref[...].astype(jnp.float32),
        (((0,), (0,)), ((), ())),
        precision=lax.Precision.HIGHEST,
        preferred_element_type=jnp.float32,
    )
    turns = exact.astype(jnp.int32) & (KG - 1)
    angle = turns.astype(jnp.float32) * (2.0 * 3.141592653589793 / KG)
    high, low = split(jnp.concatenate([jnp.cos(angle), jnp.sin(angle)], axis=0))
    return jnp.concatenate([high, high, low], axis=1)


def turn(table, block, count):
    high, low = split(block)
    both = dot(table, jnp.concatenate([high, low, high], axis=0))
    parts = []
    for at in range(0, block.shape[1], LANES):
        cos_part = both[:count, at : at + LANES]
        sin_part = pltpu.roll(both[count:, at : at + LANES], HALF, 1)
        lane = lax.broadcasted_iota(jnp.int32, sin_part.shape, 1)
        parts.append(cos_part + jnp.where(lane < HALF, -sin_part, sin_part))
    return parts


def lay_out(x_ref, o_ref, buf, held, sems):
    _, nr, modes, _, pairs = x_ref.shape
    copies = [
        pltpu.make_async_copy(x_ref.at[:, r], buf.at[r], sems.at[r]) for r in range(nr)
    ]
    for copy in copies:
        copy.start()
    held[...] = jnp.zeros_like(held)
    for r in range(nr):
        copies[r].wait()
        slot = r % 2
        held[slot, :modes] = buf[r, 0, :, 0, :]
        held[slot, HALF : HALF + modes] = buf[r, 1, :, 0, :]
        o_ref[pl.ds(r, pairs, stride=nr), :] = held[slot].T


def electron(k_ref, c_ref, x_ref, o_ref, *, kk):
    src, points = x_ref.shape[:2]
    nk = k_ref.shape[1]
    table = phases(k_ref, c_ref, kk)
    group = 8
    for start in range(0, points, group):
        cols = []
        for p in range(start, start + group):
            cols.append(jnp.concatenate([x_ref[i, p] for i in range(src)], axis=0))
        parts = turn(table, jnp.concatenate(cols, axis=1), nk)
        for t in range(group):
            o_ref[pl.ds(start + t, nk, stride=points), :] = parts[t]


def phonon(q_ref, c_ref, x_ref, o_ref):
    nq, ns = q_ref.shape[1], c_ref.shape[1]
    rows = x_ref.shape[0] // ns
    table = phases(q_ref, c_ref)
    group = 8
    for start in range(0, rows, group):
        cols = [x_ref[pl.ds(start + t, ns, stride=rows), :] for t in range(group)]
        parts = turn(table, jnp.concatenate(cols, axis=1), nq)
        for t in range(group):
            o_ref[pl.ds(start + t, nq, stride=rows), :] = parts[t]


def modes_of(x_ref, w_ref, o_ref, *, nk, pts, kk):
    owners = nk // kk
    w_high, w_low = split(w_ref[...])
    group = 9
    for start in range(0, pts, group):
        rows = []
        for p in range(start, start + group):
            both = [x_ref[pl.ds(m * pts + p, nk, stride=2 * pts), :] for m in range(2)]
            rows.append(jnp.concatenate(both, axis=1))
        high, low = split(jnp.concatenate(rows, axis=0))
        res = dot(high, w_high) + (dot(high, w_low) + dot(low, w_high))
        for t in range(group):
            for k in range(kk):
                at = t * nk + k * owners
                for m in range(2):
                    base = m * pts * kk + (start + t) * kk + k
                    o_ref[pl.ds(base, owners, stride=2 * pts * kk), :] = res[
                        at : at + owners, m * LANES : (m + 1) * LANES
                    ]


def finish(x_ref, o_ref, *, kk):
    modes, _, _, _, pairs = o_ref.shape
    for k in range(kk):
        turned = x_ref[pl.ds(k, pairs, stride=kk), :].T
        o_ref[:, 0, k, 0, :] = turned[:modes]
        o_ref[:, 0, k, 1, :] = turned[HALF : HALF + modes]


WHOLE = pl.BlockSpec(memory_space=pltpu.VMEM)
ROOM = pltpu.CompilerParams(vmem_limit_bytes=20 * 2**20)


def near(x):
    return pltpu.with_memory_space_constraint(x, pltpu.VMEM)


def call(body, rows, *args):
    return pl.pallas_call(
        body,
        out_shape=pltpu.VMEM((rows, LANES), jnp.float32),
        in_specs=[WHOLE] * len(args),
        out_specs=WHOLE,
        compiler_params=ROOM,
    )(*args)


def shards(
    coupling, electron_cells, phonon_cells, kpoint_index, qpoint_index, eigenvectors, frequencies
):
    re_size = lax.axis_size("re")
    rp_size = lax.axis_size("rp")
    _, nr, _, modes, pairs = coupling.shape
    nk = kpoint_index.shape[0]
    nq = qpoint_index.shape[0]
    ns = phonon_cells.shape[0]
    peers = re_size * 2
    pts = pairs // peers
    kk = nk // re_size

    laid = pl.pallas_call(
        lay_out,
        out_shape=pltpu.VMEM((pairs * nr, LANES), jnp.float32),
        in_specs=[pl.BlockSpec(memory_space=pltpu.HBM)],
        out_specs=WHOLE,
        compiler_params=ROOM,
        scratch_shapes=[
            pltpu.VMEM((nr, 2, modes, 1, pairs), jnp.float32),
            pltpu.VMEM((2, LANES, pairs), jnp.float32),
            pltpu.SemaphoreType.DMA((nr,)),
        ],
    )(coupling.transpose(0, 1, 3, 2, 4))
    got = exchange(laid.reshape(re_size, 2 * pts * nr, LANES), "re")
    small = (electron_cells, phonon_cells, kpoint_index, qpoint_index, eigenvectors, frequencies)
    got, small = lax.optimization_barrier((got, small))
    electron_cells, phonon_cells, kpoint_index, qpoint_index, eigenvectors, frequencies = small
    bloch_k = call(
        functools.partial(electron, kk=kk),
        nk * pts * 2,
        kpoint_index.T,
        electron_cells.T,
        near(got.reshape(re_size, 2 * pts, nr, LANES)),
    )

    packed = jnp.concatenate(
        [eigenvectors[0].reshape(2 * modes, -1), jnp.pad(frequencies, ((0, 0), (0, modes)))]
    )
    other = lax.ppermute(packed, "mode", [(0, 1), (1, 0)])
    both = jnp.stack([packed, other])
    both = jnp.where(lax.axis_index("mode") == 0, both, both[::-1])
    scale = lax.rsqrt(2.0 * both[:, -1, :modes]).reshape(-1)
    vec = both[:, :-1].reshape(2, 2, modes, 2 * modes) * scale
    real = jnp.stack([vec[:, 0], -vec[:, 1]], axis=1)
    imag = jnp.stack([vec[:, 1], vec[:, 0]], axis=1)
    weight = jnp.stack([real, imag], axis=3)
    weight = weight.reshape(2, 2, modes, 2, 2, modes).transpose(0, 1, 2, 4, 3, 5)
    gap = HALF - modes
    weight = jnp.pad(weight, ((0, 0), (0, 0), (0, gap), (0, 0), (0, 0), (0, gap)))
    weight = weight.reshape(2 * LANES, 2 * LANES)

    got = exchange(bloch_k.reshape(rp_size, pts * 2, LANES), "rp")
    bloch_kq = call(
        phonon,
        nq * pts * 2,
        qpoint_index.T,
        phonon_cells.T,
        near(got.reshape(ns * pts * 2, LANES)),
    )

    got = exchange(bloch_kq.reshape(rp_size * 2, pts // 4, 4, LANES), ("rp", "mode"))
    rotated = call(
        functools.partial(modes_of, nk=nk, pts=pts, kk=kk),
        peers * pts * kk,
        near(got.reshape(nk * pts * 2, LANES)),
        weight,
    )

    got = exchange(rotated.reshape(peers, pts * kk, LANES), ("re", "mode"))
    return pl.pallas_call(
        functools.partial(finish, kk=kk),
        out_shape=jax.ShapeDtypeStruct((modes, 1, kk, 2, pairs), jnp.float32),
        in_specs=[WHOLE],
        out_specs=WHOLE,
        compiler_params=ROOM,
    )(near(got.reshape(pairs * kk, LANES)))


def solution(mesh):
    placed = (
        P(None, "re", "rp", "mode", None),
        P(),
        P(),
        P(),
        P(),
        P("rp", None, "mode", None),
        P("rp", "mode"),
    )
    return jax.shard_map(
        shards,
        mesh=mesh,
        in_specs=placed,
        out_specs=P("mode", "rp", "re", None, None),
        check_vma=False,
    )
```

time: 125 us -> 113 us (0.904)
  blocking collectives: 15.6 us -> 51.1 us
  waiting for transfers between devices: 63.6 us -> 31.6 us
  Pallas kernels: 14.5 us -> 7.01 us
  starting transfers between devices: 24.3 us -> 18.5 us
  other arithmetic: 2.01 us -> 0.52 us
    all_to_all x1 -> x2, blocking collectives: 15.6 us -> 51.1 us  [exchange(): return lax.all_to_all(parts, axis, split_axis=0, concat_axis=0, tiled=True)]
    all_to_all x3 -> x2, waiting for transfers between devices: 63.6 us -> 31.6 us  [exchange(): return lax.all_to_all(parts, axis, split_axis=0, concat_axis=0, tiled=True)]
    pallas_call x4, Pallas kernels: 13.4 us -> 5.91 us  [the longest x3 4.1 us: call(): pl.pallas_call(body, out_shape=pltpu.VMEM((rows, LANES), jnp.float32), in...]
    all_to_all x3 -> x2, starting transfers between devices: 21.6 us -> 15.8 us  [exchange(): return lax.all_to_all(parts, axis, split_axis=0, concat_axis=0, tiled=True)]
  transfers between devices with their start and end apart: 4 -> 3, of which waited for: 3 -> 2; matrix products, arithmetic and copies ran while one was open for 4% -> 2% of each run, Pallas kernels for 2% -> 1%
where the time goes in v4:
time: 113 us; the launch traced here: 112 us
  blocking collectives  51.1 us (45%)
  waiting for transfers between devices  31.6 us (28%)
  starting transfers between devices  18.5 us (16%)
  Pallas kernels  7.01 us (6%)
  local copies, waits for them, and re-layouts  3.5 us (3%)
    all_to_all x2, blocking collectives, exchange(): return lax.all_to_all(parts, axis, split_axis=0, concat_axis=0, tiled=True)  51.1 us
    all_to_all x2, waiting for transfers between devices, exchange(): return lax.all_to_all(parts, axis, split_axis=0, concat_axis=0, tiled=True)  31.6 us
    all_to_all x2, starting transfers between devices, exchange(): return lax.all_to_all(parts, axis, split_axis=0, concat_axis=0, tiled=True)  15.8 us
    pallas_call x3, Pallas kernels, call(): pl.pallas_call(body, out_shape=pltpu.VMEM((rows, LANES), jnp.float32), in...  4.1 us
    ppermute x1, starting transfers between devices, shards(): other = lax.ppermute(packed, 'mode', [(0, 1), (1, 0)])  2.71 us
  transfers between devices with their start and end apart: 3, of which 2 were waited for; matrix products, arithmetic and copies ran while one was open for 2% of the time, Pallas kernels for 1%

profile of v4, /device:TPU:1, one launch (start us, length us, event | category | flops | bytes accessed | tf_op | source)
XLA Modules:
  0.0 112.4 jit_solution(3601768559850920768)
XLA Ops:
  0.0 1.7 %copy-done = f32[2,8,1,60,576]{4,2,3,1,0:T(1,128)S(1)} copy-done((f32[2,8,1,60,576]{4,2,3,1,0:T(1,128)S(1)}, f32[2,8,1,60,576]{4,2,3,1,0:T(1,128)}, u32[]{:S(2)}) %copy-start) | copy-done | bytes 2211864
  1.7 1.8 %shard_map.73 = f32[4608,128]{1,0:T(8,128)S(1)} custom-call(f32[2,8,60,1,576]{4,3,2,1,0:T(1,128)S(1)} %bitcast.25), custom_call_target="tpu_custom_call" | custom-call | tf_op jit(solution)/shard_map/pallas_call | solution.py:165
  3.5 0.0 copy-start.3
  3.5 0.0 copy-start.4
  3.5 34.3 %all_to_all.20 = f32[8,576,128]{2,1,0:T(8,128)S(1)} all-to-all(f32[8,576,128]{2,1,0:T(8,128)S(1)} %bitcast.24), channel_id=1, replica_groups=mesh['re'=8,'rp'=16,'mode'=2] {'re'}, dimensions={0} | all-to-all | bytes 4718592 | tf_op jit(solution)/shard_map/all_to_all | solution.py:16
  37.8 0.0 copy-done.3
  37.8 0.0 copy-done.4
  37.8 2.1 %shard_map.74 = f32[1152,128]{1,0:T(8,128)} custom-call(s32[3,16]{1,0:T(4,128)S(1)} %bitcast.32, s32[3,64]{1,0:T(4,128)S(1)} %bitcast.33, f32[8,72,8,128]{3,2,1,0:T(8,128)S(1)} %bitcast.23), custom_call_target="tpu_custom_call" | custom-call | tf_op jit(solution)/shard_map/pallas_call | solution.py:143
  40.0 10.3 %all-to-all-start.1 = ((f32[16,72,128]{2,1,0:T(8,128)}), f32[16,72,128]{2,1,0:T(8,128)S(1)}, u32[]{:S(2)}, u32[]{:S(2)}) async-start(f32[16,72,128]{2,1,0:T(8,128)} %bitcast.7), calls=%async_computation.1 | async-start | bytes 1179648 | tf_op jit(solution)/shard_map/all_to_all | solution.py:16
  50.3 0.0 copy-done.5
  50.3 0.0 copy-done.6
  50.3 2.7 %collective-permute-start = (f32[121,120]{1,0:T(8,128)S(1)}, f32[121,120]{1,0:T(8,128)S(1)}, u32[]{:S(2)}, u32[]{:S(2)}) collective-permute-start(f32[121,120]{1,0:T(8,128)S(1)} %get-tuple-element.23), channel_id=1, source_target_pairs={{0,1},{1,0},{2,3},{3,2},{4,5},{5,4},{6,7},{7,6},{8,9},{9,8},{10,11... | collective-permute-start | bytes 174248 | tf_op jit(solution)/shard_map/ppermute | solution.py:192
  53.0 15.8 %all-to-all-done.1 = f32[16,72,128]{2,1,0:T(8,128)S(1)} async-done(((f32[16,72,128]{2,1,0:T(8,128)}), f32[16,72,128]{2,1,0:T(8,128)S(1)}, u32[]{:S(2)}, u32[]{:S(2)}) %all-to-all-start.1) | async-done | bytes 589856 | tf_op jit(solution)/shard_map/all_to_all | solution.py:16
  68.8 0.0 copy-done.2
  68.8 1.5 %shard_map.75 = f32[1152,128]{1,0:T(8,128)} custom-call(s32[3,16]{1,0:T(4,128)S(1)} %bitcast.30, s32[3,16]{1,0:T(4,128)S(1)} %bitcast.31, f32[1152,128]{1,0:T(8,128)S(1)} %bitcast.27), custom_call_target="tpu_custom_call" | custom-call | tf_op jit(solution)/shard_map/pallas_call | solution.py:143
  70.3 5.5 %all-to-all-start.2 = ((f32[32,9,4,128]{3,2,1,0:T(4,128)}), f32[32,9,4,128]{3,2,1,0:T(4,128)S(1)}, u32[]{:S(2)}, u32[]{:S(2)}) async-start(f32[32,9,4,128]{3,2,1,0:T(4,128)} %bitcast.9), calls=%async_computation.2 | async-start | bytes 1179648 | tf_op jit(solution)/shard_map/all_to_all | solution.py:16
  75.9 0.0 collective-permute-done
  75.9 0.1 copy.19
  76.0 0.1 rsqrt.11
  76.2 0.1 pad_maximum_fusion.1
  76.4 0.1 copy.20
  76.4 0.2 stack.29
  76.7 0.1 copy.21
  76.7 0.2 stack.31
  77.0 0.3 maximum_bitcast_fusion
  77.2 0.4 copy.24
  77.6 0.2 pad.9.clone
  77.8 0.5 reshape.51.w_ref
  78.3 15.8 %all-to-all-done.2 = f32[32,9,4,128]{3,2,1,0:T(4,128)S(1)} async-done(((f32[32,9,4,128]{3,2,1,0:T(4,128)}), f32[32,9,4,128]{3,2,1,0:T(4,128)S(1)}, u32[]{:S(2)}, u32[]{:S(2)}) %all-to-all-start.2) | async-done | bytes 589856 | tf_op jit(solution)/shard_map/all_to_all | solution.py:16
  94.1 0.4 shard_map.76
  94.5 16.8 %all_to_all.21 = f32[16,72,128]{2,1,0:T(8,128)S(1)} all-to-all(f32[16,72,128]{2,1,0:T(8,128)S(1)} %bitcast.28), channel_id=1, replica_groups=mesh['re'=8,'rp'=16,'mode'=2] {'re','mode'}, dimensions={0} | all-to-all | bytes 1179648 | tf_op jit(solution)/shard_map/all_to_all | solution.py:16
  111.3 1.1 shard_map.77
  (15 shorter events, 0.2 us)
Async XLA Ops:
  0.0 1.7 %copy-start = (f32[2,8,1,60,576]{4,2,3,1,0:T(1,128)S(1)}, f32[2,8,1,60,576]{4,2,3,1,0:T(1,128)}, u32[]{:S(2)}) copy-start(f32[2,8,1,60,576]{4,2,3,1,0:T(1,128)} %param.7) | copy-start | bytes 6635524
  3.5 34.3 %copy-start.3 = (s32[16,3]{0,1:T(4,128)S(1)}, s32[16,3]{0,1:T(4,128)}, u32[]{:S(2)}) copy-start(s32[16,3]{0,1:T(4,128)} %param.10) | copy-start | bytes 580
  3.5 34.3 %copy-start.4 = (s32[64,3]{0,1:T(4,128)S(1)}, s32[64,3]{0,1:T(4,128)}, u32[]{:S(2)}) copy-start(s32[64,3]{0,1:T(4,128)} %param.8) | copy-start | bytes 2308
  37.8 12.4 %copy-start.5 = (f32[1,2,60,120]{3,1,2,0:T(2,128)S(1)}, f32[1,2,60,120]{3,1,2,0:T(2,128)}, u32[]{:S(2)}) copy-start(f32[1,2,60,120]{3,1,2,0:T(2,128)} %param.12) | copy-start | bytes 172804
  37.8 12.5 %copy-start.6 = (f32[1,60]{1,0:T(1,128)S(1)}, f32[1,60]{1,0:T(1,128)}, u32[]{:S(2)}) copy-start(f32[1,60]{1,0:T(1,128)} %param.13) | copy-start | bytes 724
  37.8 31.0 %copy-start.1 = (s32[16,3]{0,1:T(4,128)S(1)}, s32[16,3]{0,1:T(4,128)}, u32[]{:S(2)}) copy-start(s32[16,3]{0,1:T(4,128)} %param.11) | copy-start | bytes 580
  37.8 31.0 %copy-start.2 = (s32[16,3]{0,1:T(4,128)S(1)}, s32[16,3]{0,1:T(4,128)}, u32[]{:S(2)}) copy-start(s32[16,3]{0,1:T(4,128)} %param.9) | copy-start | bytes 580
  40.0 28.8 %all-to-all-start.1 = ((f32[16,72,128]{2,1,0:T(8,128)}), f32[16,72,128]{2,1,0:T(8,128)S(1)}, u32[]{:S(2)}, u32[]{:S(2)}) async-start(f32[16,72,128]{2,1,0:T(8,128)} %bitcast.7), calls=%async_computation.1 | async-start | bytes 1179648 | tf_op jit(solution)/shard_map/all_to_all | solution.py:16
  50.3 25.5 %collective-permute-start = (f32[121,120]{1,0:T(8,128)S(1)}, f32[121,120]{1,0:T(8,128)S(1)}, u32[]{:S(2)}, u32[]{:S(2)}) collective-permute-start(f32[121,120]{1,0:T(8,128)S(1)} %get-tuple-element.23), channel_id=1, source_target_pairs={{0,1},{1,0},{2,3},{3,2},{4,5},{5,4},{6,7},{7,6},{8,9},{9,8},{10,11... | collective-permute-start | bytes 174248 | tf_op jit(solution)/shard_map/ppermute | solution.py:192
  70.3 23.8 %all-to-all-start.2 = ((f32[32,9,4,128]{3,2,1,0:T(4,128)}), f32[32,9,4,128]{3,2,1,0:T(4,128)S(1)}, u32[]{:S(2)}, u32[]{:S(2)}) async-start(f32[32,9,4,128]{3,2,1,0:T(4,128)} %bitcast.9), calls=%async_computation.2 | async-start | bytes 1179648 | tf_op jit(solution)/shard_map/all_to_all | solution.py:16

commit v5 on v4

--- a/solution.py
+++ b/solution.py
@@ -60,26 +60,35 @@
     return parts
 
 
-def lay_out(x_ref, o_ref, buf, held, sems):
+def lay_out(x_ref, *refs, kk):
+    o_ref, e_ref, p_ref, buf, held, sems, small_sems = refs[4:11]
     _, nr, modes, _, pairs = x_ref.shape
+    small = [
+        pltpu.make_async_copy(refs[i], refs[11 + i], small_sems.at[i]) for i in range(4)
+    ]
     copies = [
         pltpu.make_async_copy(x_ref.at[:, r], buf.at[r], sems.at[r]) for r in range(nr)
     ]
-    for copy in copies:
+    for copy in copies[:1] + small + copies[1:]:
         copy.start()
     held[...] = jnp.zeros_like(held)
     for r in range(nr):
         copies[r].wait()
+        if r == nr // 2:
+            for copy in small:
+                copy.wait()
+            e_ref[...] = phases(refs[11], refs[12], kk)
+            p_ref[...] = phases(refs[13], refs[14])
         slot = r % 2
         held[slot, :modes] = buf[r, 0, :, 0, :]
         held[slot, HALF : HALF + modes] = buf[r, 1, :, 0, :]
         o_ref[pl.ds(r, pairs, stride=nr), :] = held[slot].T
 
 
-def electron(k_ref, c_ref, x_ref, o_ref, *, kk):
+def electron(t_ref, x_ref, o_ref):
     src, points = x_ref.shape[:2]
-    nk = k_ref.shape[1]
-    table = phases(k_ref, c_ref, kk)
+    nk = t_ref.shape[0] // 2
+    table = t_ref[...]
     group = 8
     for start in range(0, points, group):
         cols = []
@@ -90,10 +99,10 @@
             o_ref[pl.ds(start + t, nk, stride=points), :] = parts[t]
 
 
-def phonon(q_ref, c_ref, x_ref, o_ref):
-    nq, ns = q_ref.shape[1], c_ref.shape[1]
+def phonon(t_ref, x_ref, o_ref):
+    nq, ns = t_ref.shape[0] // 2, t_ref.shape[1] // 3
     rows = x_ref.shape[0] // ns
-    table = phases(q_ref, c_ref)
+    table = t_ref[...]
     group = 8
     for start in range(0, rows, group):
         cols = [x_ref[pl.ds(start + t, ns, stride=rows), :] for t in range(group)]
@@ -131,8 +140,13 @@
         o_ref[:, 0, k, 1, :] = turned[HALF : HALF + modes]
 
 
+FAR = pl.BlockSpec(memory_space=pltpu.HBM)
 WHOLE = pl.BlockSpec(memory_space=pltpu.VMEM)
 ROOM = pltpu.CompilerParams(vmem_limit_bytes=20 * 2**20)
+
+
+def far(x):
+    return pltpu.with_memory_space_constraint(x, pltpu.HBM)
 
 
 def near(x):
@@ -162,27 +176,31 @@
     pts = pairs // peers
     kk = nk // re_size
 
-    laid = pl.pallas_call(
-        lay_out,
-        out_shape=pltpu.VMEM((pairs * nr, LANES), jnp.float32),
-        in_specs=[pl.BlockSpec(memory_space=pltpu.HBM)],
-        out_specs=WHOLE,
+    tables = [x.T for x in (kpoint_index, electron_cells, qpoint_index, phonon_cells)]
+    laid, table_e, table_p = pl.pallas_call(
+        functools.partial(lay_out, kk=kk),
+        out_shape=[
+            pltpu.VMEM((pairs * nr, LANES), jnp.float32),
+            pltpu.VMEM((2 * nk, 3 * re_size * nr), jnp.bfloat16),
+            pltpu.VMEM((2 * nq, 3 * ns), jnp.bfloat16),
+        ],
+        in_specs=[FAR] * 5,
+        out_specs=[WHOLE] * 3,
         compiler_params=ROOM,
         scratch_shapes=[
             pltpu.VMEM((nr, 2, modes, 1, pairs), jnp.float32),
             pltpu.VMEM((2, LANES, pairs), jnp.float32),
             pltpu.SemaphoreType.DMA((nr,)),
-        ],
-    )(coupling.transpose(0, 1, 3, 2, 4))
+            pltpu.SemaphoreType.DMA((4,)),
+        ]
+        + [pltpu.VMEM(x.shape, x.dtype) for x in tables],
+    )(far(coupling.transpose(0, 1, 3, 2, 4)), *[far(x) for x in tables])
     got = exchange(laid.reshape(re_size, 2 * pts * nr, LANES), "re")
-    small = (electron_cells, phonon_cells, kpoint_index, qpoint_index, eigenvectors, frequencies)
-    got, small = lax.optimization_barrier((got, small))
-    electron_cells, phonon_cells, kpoint_index, qpoint_index, eigenvectors, frequencies = small
+    got, eigenvectors, frequencies = lax.optimization_barrier((got, eigenvectors, frequencies))
     bloch_k = call(
-        functools.partial(electron, kk=kk),
+        electron,
         nk * pts * 2,
-        kpoint_index.T,
-        electron_cells.T,
+        table_e,
         near(got.reshape(re_size, 2 * pts, nr, LANES)),
     )
 
@@ -206,8 +224,7 @@
     bloch_kq = call(
         phonon,
         nq * pts * 2,
-        qpoint_index.T,
-        phonon_cells.T,
+        table_p,
         near(got.reshape(ns * pts * 2, LANES)),
     )
 

time: 113 us -> 111 us (0.982)
  local copies, waits for them, and re-layouts: 3.5 us -> 1.78 us
    unnamed x15 -> x5, local copies, waits for them, and re-layouts: 2.1 us -> 0.39 us
where the time goes in v5:
time: 111 us
  blocking collectives  51.1 us (46%)
  waiting for transfers between devices  31.6 us (28%)
  starting transfers between devices  18.5 us (17%)
  Pallas kernels  7.25 us (7%)
  local copies, waits for them, and re-layouts  1.78 us (2%)
    all_to_all x2, blocking collectives, exchange(): return lax.all_to_all(parts, axis, split_axis=0, concat_axis=0, tiled=True)  51.1 us
    all_to_all x2, waiting for transfers between devices, exchange(): return lax.all_to_all(parts, axis, split_axis=0, concat_axis=0, tiled=True)  31.6 us
    all_to_all x2, starting transfers between devices, exchange(): return lax.all_to_all(parts, axis, split_axis=0, concat_axis=0, tiled=True)  15.8 us
    pallas_call x3, Pallas kernels, call(): pl.pallas_call(body, out_shape=pltpu.VMEM((rows, LANES), jnp.float32), in...  3.31 us
    pallas_call x1, Pallas kernels, shards(): pl.pallas_call(functools.partial(lay_out, kk=kk), out_shape=[pltpu.VMEM((...  2.84 us
    ppermute x1, starting transfers between devices, shards(): other = lax.ppermute(packed, 'mode', [(0, 1), (1, 0)])  2.71 us
  transfers between devices with their start and end apart: 3, of which 2 were waited for; matrix products, arithmetic and copies ran while one was open for 2% of the time, Pallas kernels for 1%

profile of v5, /device:TPU:1, one launch (start us, length us, event | category | flops | bytes accessed | tf_op | source)
XLA Modules:
  0.0 110.9 jit_solution(4537770420924866364)
XLA Ops:
  0.0 2.8 %shard_map.73 = (f32[4608,128]{1,0:T(8,128)S(1)}, bf16[32,192]{1,0:T(8,128)(2,1)S(1)}, bf16[32,48]{1,0:T(8,128)(2,1)S(1)}) custom-call(f32[2,8,60,1,576]{4,3,2,1,0:T(1,128)} %bitcast.29, s32[3,16]{1,0:T(4,128)} %bitcast.32, s32[3,64]{1,0:T(4,128)} %bitcast.33, s32[3,16]{1,0:T(4,128)} %bitcast.34, s32[3,16]{1,0:T(4,128)} %bitcast.35), custom_call_target="tpu_custom_call" | custom-call | tf_op jit(solution)/shard_map/pallas_call | solution.py:180
  2.8 34.3 %all_to_all.20 = f32[8,576,128]{2,1,0:T(8,128)S(1)} all-to-all(f32[8,576,128]{2,1,0:T(8,128)S(1)} %bitcast.24), channel_id=1, replica_groups=mesh['re'=8,'rp'=16,'mode'=2] {'re'}, dimensions={0} | all-to-all | bytes 4718592 | tf_op jit(solution)/shard_map/all_to_all | solution.py:16
  37.1 0.0 copy-start
  37.1 0.0 copy-start.1
  37.1 1.7 %shard_map.74 = f32[1152,128]{1,0:T(8,128)} custom-call(bf16[32,192]{1,0:T(8,128)(2,1)S(1)} %get-tuple-element.12.t_ref, f32[8,72,8,128]{3,2,1,0:T(8,128)S(1)} %bitcast.23), custom_call_target="tpu_custom_call" | custom-call | tf_op jit(solution)/shard_map/pallas_call | solution.py:157
  38.8 10.3 %all-to-all-start.1 = ((f32[16,72,128]{2,1,0:T(8,128)}), f32[16,72,128]{2,1,0:T(8,128)S(1)}, u32[]{:S(2)}, u32[]{:S(2)}) async-start(f32[16,72,128]{2,1,0:T(8,128)} %bitcast.7), calls=%async_computation.1 | async-start | bytes 1179648 | tf_op jit(solution)/shard_map/all_to_all | solution.py:16
  49.1 0.0 copy-done
  49.1 0.0 copy-done.1
  49.1 2.7 %collective-permute-start = (f32[121,120]{1,0:T(8,128)S(1)}, f32[121,120]{1,0:T(8,128)S(1)}, u32[]{:S(2)}, u32[]{:S(2)}) collective-permute-start(f32[121,120]{1,0:T(8,128)S(1)} %get-tuple-element.21), channel_id=1, source_target_pairs={{0,1},{1,0},{2,3},{3,2},{4,5},{5,4},{6,7},{7,6},{8,9},{9,8},{10,11... | collective-permute-start | bytes 174248 | tf_op jit(solution)/shard_map/ppermute | solution.py:210
  51.9 15.8 %all-to-all-done.1 = f32[16,72,128]{2,1,0:T(8,128)S(1)} async-done(((f32[16,72,128]{2,1,0:T(8,128)}), f32[16,72,128]{2,1,0:T(8,128)S(1)}, u32[]{:S(2)}, u32[]{:S(2)}) %all-to-all-start.1) | async-done | bytes 589856 | tf_op jit(solution)/shard_map/all_to_all | solution.py:16
  67.6 1.2 %shard_map.75 = f32[1152,128]{1,0:T(8,128)} custom-call(bf16[32,48]{1,0:T(8,128)(2,1)S(1)} %get-tuple-element.11.t_ref, f32[1152,128]{1,0:T(8,128)S(1)} %bitcast.26), custom_call_target="tpu_custom_call" | custom-call | tf_op jit(solution)/shard_map/pallas_call | solution.py:157
  68.8 5.5 %all-to-all-start.2 = ((f32[32,9,4,128]{3,2,1,0:T(4,128)}), f32[32,9,4,128]{3,2,1,0:T(4,128)S(1)}, u32[]{:S(2)}, u32[]{:S(2)}) async-start(f32[32,9,4,128]{3,2,1,0:T(4,128)} %bitcast.9), calls=%async_computation.2 | async-start | bytes 1179648 | tf_op jit(solution)/shard_map/all_to_all | solution.py:16
  74.4 0.0 collective-permute-done
  74.4 0.1 copy.19
  74.5 0.1 rsqrt.11
  74.7 0.1 pad_maximum_fusion.1
  74.8 0.1 copy.21
  74.9 0.2 stack.31
  75.1 0.1 copy.20
  75.2 0.2 stack.29
  75.5 0.3 maximum_bitcast_fusion
  75.7 0.4 copy.24
  76.1 0.2 pad.9.clone
  76.3 0.5 reshape.51.w_ref
  76.7 15.8 %all-to-all-done.2 = f32[32,9,4,128]{3,2,1,0:T(4,128)S(1)} async-done(((f32[32,9,4,128]{3,2,1,0:T(4,128)}), f32[32,9,4,128]{3,2,1,0:T(4,128)S(1)}, u32[]{:S(2)}, u32[]{:S(2)}) %all-to-all-start.2) | async-done | bytes 589856 | tf_op jit(solution)/shard_map/all_to_all | solution.py:16
  92.6 0.4 shard_map.76
  93.0 16.8 %all_to_all.21 = f32[16,72,128]{2,1,0:T(8,128)S(1)} all-to-all(f32[16,72,128]{2,1,0:T(8,128)S(1)} %bitcast.27), channel_id=1, replica_groups=mesh['re'=8,'rp'=16,'mode'=2] {'re','mode'}, dimensions={0} | all-to-all | bytes 1179648 | tf_op jit(solution)/shard_map/all_to_all | solution.py:16
  109.8 1.1 shard_map.77
  (9 shorter events, 0.2 us)
Async XLA Ops:
  37.1 12.0 %copy-start = (f32[1,2,60,120]{3,1,2,0:T(2,128)S(1)}, f32[1,2,60,120]{3,1,2,0:T(2,128)}, u32[]{:S(2)}) copy-start(f32[1,2,60,120]{3,1,2,0:T(2,128)} %param.12) | copy-start | bytes 172804
  37.1 12.0 %copy-start.1 = (f32[1,60]{1,0:T(1,128)S(1)}, f32[1,60]{1,0:T(1,128)}, u32[]{:S(2)}) copy-start(f32[1,60]{1,0:T(1,128)} %param.13) | copy-start | bytes 724
  38.8 28.8 %all-to-all-start.1 = ((f32[16,72,128]{2,1,0:T(8,128)}), f32[16,72,128]{2,1,0:T(8,128)S(1)}, u32[]{:S(2)}, u32[]{:S(2)}) async-start(f32[16,72,128]{2,1,0:T(8,128)} %bitcast.7), calls=%async_computation.1 | async-start | bytes 1179648 | tf_op jit(solution)/shard_map/all_to_all | solution.py:16
  49.1 25.2 %collective-permute-start = (f32[121,120]{1,0:T(8,128)S(1)}, f32[121,120]{1,0:T(8,128)S(1)}, u32[]{:S(2)}, u32[]{:S(2)}) collective-permute-start(f32[121,120]{1,0:T(8,128)S(1)} %get-tuple-element.21), channel_id=1, source_target_pairs={{0,1},{1,0},{2,3},{3,2},{4,5},{5,4},{6,7},{7,6},{8,9},{9,8},{10,11... | collective-permute-start | bytes 174248 | tf_op jit(solution)/shard_map/ppermute | solution.py:210
  68.8 23.8 %all-to-all-start.2 = ((f32[32,9,4,128]{3,2,1,0:T(4,128)}), f32[32,9,4,128]{3,2,1,0:T(4,128)S(1)}, u32[]{:S(2)}, u32[]{:S(2)}) async-start(f32[32,9,4,128]{3,2,1,0:T(4,128)} %bitcast.9), calls=%async_computation.2 | async-start | bytes 1179648 | tf_op jit(solution)/shard_map/all_to_all | solution.py:16
